TPU v7x, 256 devices: a whole 4x4x8 slice. The times are simulated.
256 devices in a mesh: art: 64 (over z, y, core), seq: 4 (over x).
Axes of the slice: x: 4, y: 4, z: 8, core: 2. Of those that a mesh axis runs over, the one named last changes fastest.
Arguments:
- queries: bfloat16 [768, 4, 256, 128], P('art', 'seq'), may hold values from -6 to 6
- cand_owner: int32 [3072, 16, 4], P(('art', 'seq')), may hold values from 0 to 63, all different within a row; in each aligned block of 192 rows (0 to 191, 192 to 383, ..., all dimensions but the last counted through in order) at most 18 rows name the same one
- cand_local: int32 [3072, 16, 4], P(('art', 'seq')), may hold values from 0 to 255, as said below
- companies: bfloat16 [16384, 64, 128], P('art'), may hold values from -6 to 6
Outputs:
- relevance: float32 [3072, 64], P(('art', 'seq'))
- probs: float32 [3072, 64], P(('art', 'seq'))
Inputs may be any that keep to these rules, and one draw needn't show every extreme that they name: `cand_owner`: each row of four candidates names four different owners. Among the candidates of one device's 12 articles (aligned blocks of 12 articles in the order of the array), no owner is named more than 18 times, a bound that some block reaches. `cand_local`: the candidates of one device's 12 articles (aligned blocks of 12 articles in the order of the array) name exactly 9 different local indices in all.
All inputs are finite; a program needn't handle non-finite values.
Results may differ from a plain program's by a relative error of at most 0.0088.
Values may be sent and summed in bfloat16 or wider, within the bound.
A program may use at most 128 MiB of HBM per device.

v0:
```python
import jax
import jax.numpy as jnp
from jax import lax
from jax.sharding import PartitionSpec as P

LC = 64
NC = 64


EPS = 1e-06
SHARP = 16.0
TEMPER = 4.0


def unit_rows(values):
    wide = values.astype(jnp.float32)
    return (wide * lax.rsqrt(jnp.sum(wide * wide, axis=-1, keepdims=True) + EPS)).astype(
        jnp.bfloat16
    )


def pool_pair(pair):
    query_pair, block_pair = pair
    sims = jnp.einsum("aqe,ake->aqk", query_pair, block_pair, preferred_element_type=jnp.float32)
    count = query_pair.shape[0]
    tokens = query_pair.shape[1]
    mass = jnp.sum(jnp.exp(sims * SHARP).reshape(count, tokens, NC, LC), axis=-1)
    return jnp.sum(jnp.log(mass), axis=1) / SHARP


def owner_ranks(owner_table, marks):
    return jnp.sum(jnp.cumsum(owner_table * marks[:, None], axis=0) * owner_table, axis=1) - 1


def per_device(queries, cand_owner, cand_local, companies):
    moved = lax.all_to_all(queries, "seq", split_axis=0, concat_axis=1, tiled=True)
    mine = moved.reshape(-1, moved.shape[2], moved.shape[3])
    query_unit = unit_rows(mine)
    catalog = unit_rows(companies)
    articles = mine.shape[0]
    width = mine.shape[2]
    owners = cand_owner.reshape(-1)
    local_ids = cand_local.reshape(-1)
    request_count = owners.shape[0]
    owner_count = lax.axis_size("art")
    cap_slots = 3 * request_count // (2 * owner_count)
    owner_table = (owners[:, None] == jnp.arange(owner_count, dtype=jnp.int32)[None, :]).astype(
        jnp.int32
    )
    every_one = jnp.ones((request_count,), jnp.int32)
    slot_index = owner_ranks(owner_table, every_one)
    table = jnp.zeros((owner_count, cap_slots), jnp.int32).at[owners, slot_index].set(local_ids)
    arrived = lax.all_to_all(
        catalog[lax.all_to_all(table, "art", split_axis=0, concat_axis=0, tiled=True)],
        "art",
        split_axis=0,
        concat_axis=0,
        tiled=True,
    )
    chosen = arrived[owners, slot_index]
    blocks = chosen.reshape(articles // 2, 2, NC * LC, width)
    query_pairs = query_unit.reshape(articles // 2, 2, query_unit.shape[1], width)
    score = lax.map(pool_pair, (query_pairs, blocks)).reshape(articles, NC)
    relevance = score - jnp.mean(score, axis=-1, keepdims=True)
    weights = jnp.exp(TEMPER * relevance)
    probs = weights / jnp.sum(weights, axis=-1, keepdims=True)
    return (relevance, probs)


def solution(mesh):
    placed = (
        P("art", "seq", None, None),
        P(("art", "seq"), None, None),
        P(("art", "seq"), None, None),
        P("art", None, None),
    )
    return jax.shard_map(
        per_device,
        mesh=mesh,
        in_specs=placed,
        out_specs=(P(("art", "seq"), None), P(("art", "seq"), None)),
        check_vma=False,
    )
```

profile of v0, /device:TPU:1, one launch (start us, length us, event | category | flops | bytes accessed | tf_op | source)
XLA Modules:
  0.0 657.4 jit_solution(16596891297023123141)
XLA Ops:
  0.6 0.9 copy.27
  1.5 0.1 eq.29
  1.6 0.1 eq.25
  1.7 0.1 reshape.173
  1.9 1.8 reduce-window.6
  3.7 0.3 slice_reduce_fusion
  4.0 0.1 fusion.8
  4.1 0.9 copy.31
  5.0 0.1 reshape.199
  5.2 37.5 %scatter_fusion = s32[64,18]{0,1:T(8,128)S(1)} fusion(s32[64,18]{0,1:T(8,128)S(1)} %broadcast.129, s32[768]{0:T(1024)S(1)} %get-tuple-element.26, s32[768]{0:T(1024)S(1)} %reshape.199), kind=kCustom, calls=%fused_computation.2 | custom fusion | bytes 15360 | tf_op jit(solution)/shard_map/scatter | solution.py:52
  42.6 0.7 copy.32
  43.3 13.2 %all-to-all-start.1 = ((s32[64,1,18]{2,1,0:T(1,128)}), s32[64,1,18]{2,1,0:T(1,128)S(1)}, u32[]{:S(2)}, u32[]{:S(2)}) async-start(s32[64,1,18]{2,1,0:T(1,128)} %copy.32), calls=%async_computation.1 | async-start | bytes 65536 | tf_op jit(solution)/shard_map/all_to_all | solution.py:54
  56.5 4.4 fusion.5
  61.0 4.9 all-to-all-done.1
  65.9 4.0 all-to-all-start
  69.9 5.8 fusion.6
  75.7 0.1 reshape.185
  75.8 28.4 %gather_fusion = bf16[1152,64,128]{2,1,0:T(8,128)(2,1)} fusion(bf16[256,64,128]{2,1,0:T(8,128)(2,1)} %fusion.6, s32[2048]{0:T(1024)S(1)} %pad_clamp_fusion), kind=kCustom, calls=%fused_computation | custom fusion | bytes 37753344 | tf_op jit(solution)/shard_map/gather | solution.py:54
  104.2 0.0 all-to-all-done
  104.2 6.6 %all-to-all-start.2 = ((bf16[64,18,64,128]{3,2,1,0:T(8,128)(2,1)}), bf16[64,18,64,128]{3,2,1,0:T(8,128)(2,1)}, u32[]{:S(2)}, u32[]{:S(2)}) async-start(bf16[64,18,64,128]{3,2,1,0:T(8,128)(2,1)} %bitcast.47), calls=%async_computation.2 | async-start | bytes 37748736 | tf_op jit(solution)/shard_map/all_to_all | solution.py:53
  110.9 0.1 copy.25
  111.0 0.5 multiply_reduce_fusion
  111.6 0.5 multiply_convert_fusion
  112.0 410.6 %all-to-all-done.2 = bf16[64,18,64,128]{3,2,1,0:T(8,128)(2,1)} async-done(((bf16[64,18,64,128]{3,2,1,0:T(8,128)(2,1)}), bf16[64,18,64,128]{3,2,1,0:T(8,128)(2,1)}, u32[]{:S(2)}, u32[]{:S(2)}) %all-to-all-start.2) | async-done | bytes 18874400 | tf_op jit(solution)/shard_map/all_to_all | solution.py:53
  522.7 15.1 %gather_fusion.1 = bf16[768,64,128]{2,1,0:T(8,128)(2,1)} fusion(bf16[64,18,64,128]{3,2,1,0:T(8,128)(2,1)} %all-to-all-done.2, s32[768]{0:T(1024)S(1)} %get-tuple-element.25), kind=kCustom, calls=%fused_computation.1 | custom fusion | bytes 25171968 | tf_op jit(solution)/shard_map/gather | solution.py:60
  537.7 118.5 %while.10 = (s32[]{:T(128)}, f32[6,2,64]{2,1,0:T(2,128)S(1)}, bf16[6,2,256,128]{3,2,1,0:T(8,128)(2,1)S(1)}, bf16[6,2,4096,128]{3,2,1,0:T(8,128)(2,1)}, s32[]{:T(128)}) while((s32[]{:T(128)}, f32[6,2,64]{2,1,0:T(2,128)S(1)}, bf16[6,2,256,128]{3,2,1,0:T(8,128)(2,1)S(1)}, bf16[6,2,4096,128]{3,2,1,0:T(8,128)(2,1)}, s32[]{:T(128)}) %tuple.28), condition=%wide.region_9.10_spmd, body=%wide.region_6.9_spmd.sunk | while | flops 541065216 | bytes 36048448 | solution.py:63
  537.7 6.1 multiply_exponential_fusion.2
  543.8 8.9 %copy.36 = f32[2,256,4096]{1,2,0:T(8,128)} copy(f32[2,256,4096]{2,1,0:T(8,128)} %multiply_exponential_fusion.2) | data formatting | bytes 16777216 | tf_op jit(solution)/shard_map/while/body/eval_jaxpr/exp | solution.py:27
  552.7 4.6 bitcast_reduce_fusion.2
  557.3 0.1 log_reduce_fusion.2
  557.5 6.1 multiply_exponential_fusion.2
  563.5 8.9 %copy.36 = f32[2,256,4096]{1,2,0:T(8,128)} copy(f32[2,256,4096]{2,1,0:T(8,128)} %multiply_exponential_fusion.2) | data formatting | bytes 16777216 | tf_op jit(solution)/shard_map/while/body/eval_jaxpr/exp | solution.py:27
  572.5 4.6 bitcast_reduce_fusion.2
  577.1 0.1 log_reduce_fusion.2
  577.2 6.1 multiply_exponential_fusion.2
  583.3 8.9 %copy.36 = f32[2,256,4096]{1,2,0:T(8,128)} copy(f32[2,256,4096]{2,1,0:T(8,128)} %multiply_exponential_fusion.2) | data formatting | bytes 16777216 | tf_op jit(solution)/shard_map/while/body/eval_jaxpr/exp | solution.py:27
  592.2 4.6 bitcast_reduce_fusion.2
  596.9 0.1 log_reduce_fusion.2
  597.0 6.1 multiply_exponential_fusion.2
  603.1 8.9 %copy.36 = f32[2,256,4096]{1,2,0:T(8,128)} copy(f32[2,256,4096]{2,1,0:T(8,128)} %multiply_exponential_fusion.2) | data formatting | bytes 16777216 | tf_op jit(solution)/shard_map/while/body/eval_jaxpr/exp | solution.py:27
  612.0 4.6 bitcast_reduce_fusion.2
  616.6 0.1 log_reduce_fusion.2
  616.8 6.1 multiply_exponential_fusion.2
  622.8 8.9 %copy.36 = f32[2,256,4096]{1,2,0:T(8,128)} copy(f32[2,256,4096]{2,1,0:T(8,128)} %multiply_exponential_fusion.2) | data formatting | bytes 16777216 | tf_op jit(solution)/shard_map/while/body/eval_jaxpr/exp | solution.py:27
  631.7 4.6 bitcast_reduce_fusion.2
  636.4 0.1 log_reduce_fusion.2
  636.5 6.1 multiply_exponential_fusion.2
  642.6 8.9 %copy.36 = f32[2,256,4096]{1,2,0:T(8,128)} copy(f32[2,256,4096]{2,1,0:T(8,128)} %multiply_exponential_fusion.2) | data formatting | bytes 16777216 | tf_op jit(solution)/shard_map/while/body/eval_jaxpr/exp | solution.py:27
  651.5 4.6 bitcast_reduce_fusion.2
  656.1 0.1 log_reduce_fusion.2
  656.3 0.1 reduce_sum.69
  656.4 0.2 exponential_reduce_fusion
  656.5 0.1 div.21
  656.6 0.1 div.22
  656.7 0.7 exponential_divide_fusion
  (21 shorter events, 0.3 us)
Async XLA Ops:
  43.3 22.5 %all-to-all-start.1 = ((s32[64,1,18]{2,1,0:T(1,128)}), s32[64,1,18]{2,1,0:T(1,128)S(1)}, u32[]{:S(2)}, u32[]{:S(2)}) async-start(s32[64,1,18]{2,1,0:T(1,128)} %copy.32), calls=%async_computation.1 | async-start | bytes 65536 | tf_op jit(solution)/shard_map/all_to_all | solution.py:54
  65.9 38.4 %all-to-all-start = ((bf16[12,1,256,128]{3,2,1,0:T(8,128)(2,1)}), bf16[12,1,256,128]{3,2,1,0:T(8,128)(2,1)S(1)}, u32[]{:S(2)}, u32[]{:S(2)}) async-start(bf16[12,1,256,128]{3,2,1,0:T(8,128)(2,1)} %param.6), calls=%async_computation | async-start | bytes 1572864 | tf_op jit(solution)/shard_map/all_to_all | solution.py:36
  104.2 418.4 %all-to-all-start.2 = ((bf16[64,18,64,128]{3,2,1,0:T(8,128)(2,1)}), bf16[64,18,64,128]{3,2,1,0:T(8,128)(2,1)}, u32[]{:S(2)}, u32[]{:S(2)}) async-start(bf16[64,18,64,128]{3,2,1,0:T(8,128)(2,1)} %bitcast.47), calls=%async_computation.2 | async-start | bytes 37748736 | tf_op jit(solution)/shard_map/all_to_all | solution.py:53
where the time goes:
time: 667 us; the launch traced here: 657 us
  waiting for transfers between devices  416 us (62%)
  local copies, waits for them, and re-layouts  138 us (21%)
  other arithmetic  42.7 us (6%)
  matrix products  36.4 us (5%)
  starting transfers between devices  23.8 us (4%)
    all_to_all x1, waiting for transfers between devices, per_device(): lax.all_to_all(catalog[lax.all_to_all(table, 'art', split_axis=0, concat_...  411 us
    exp x6, local copies, waits for them, and re-layouts, pool_pair(): jnp.exp(sims * SHARP).reshape(count, tokens, NC, LC)  53.5 us
    scatter x1, local copies, waits for them, and re-layouts, per_device(): jnp.zeros((owner_count, cap_slots), jnp.int32).at[owners, slot_index]  37.5 us
    dot_general x6, matrix products, pool_pair(): jnp.einsum('aqe,ake->aqk', query_pair, block_pair, preferred_element_type...  36.4 us
    gather x1, local copies, waits for them, and re-layouts, per_device(): catalog[lax.all_to_all(table, 'art', split_axis=0, concat_axis=0, tiled=T...  28.4 us
    reduce_sum x6, other arithmetic, pool_pair(): jnp.sum(jnp.exp(sims * SHARP).reshape(count, tokens, NC, LC), axis=-1)  27.7 us
    gather x1, local copies, waits for them, and re-layouts, per_device(): chosen = arrived[owners, slot_index]  15.1 us
  transfers between devices with their start and end apart: 3, of which 2 were waited for; matrix products, arithmetic and copies ran while one was open for 6% of the time, Pallas kernels for 0%

commit v1 on v0

v1 whole, which is shorter than its diff:
```python
import math

import jax
import jax.numpy as jnp
from jax import lax
from jax.experimental import pallas as pl
from jax.experimental.pallas import tpu as pltpu
from jax.sharding import PartitionSpec as P

EPS = 1e-06
SHARP = 16.0
TEMPER = 4.0
MESH = pl.DeviceIdType.MESH
HBM = pl.BlockSpec(memory_space=pl.ANY)
VMEM = pl.BlockSpec(memory_space=pltpu.VMEM)

NX, NY, NZ = 4, 4, 8
ARTS = 12
PART = ARTS // NX
LQ, LC, E = 256, 64, 128
NC = 64
C_DEV = 256
CAP = 18
SLOTS = NY * CAP
GROUPS = SLOTS // 8
WORKERS = NZ * 2
REQ = ARTS * NC
SPLIT = 160
QUARTER = SPLIT // NX
HALF = QUARTER // 2
REST = (C_DEV - SPLIT) // 2


def unit(values):
    wide = values.astype(jnp.float32)
    return wide * lax.rsqrt(jnp.sum(wide * wide, axis=-1, keepdims=True) + EPS)


def place():
    art, x = lax.axis_index("art"), lax.axis_index("seq")
    return art // (NY * 2), (art // 2) % NY, art % 2, x


def prepare_kernel(own_ref, loc_ref, q_ref, c_ref, qt_ref, cat_ref, list_ref, slot_ref):
    def normalise(i, carry):
        cat_ref[pl.ds(i * 8, 8)] = unit(c_ref[pl.ds(i * 8, 8)]).astype(jnp.bfloat16)
        return carry

    lax.fori_loop(0, c_ref.shape[0] // 8, normalise, 0)
    for a in range(PART):
        qt_ref[a] = jnp.transpose(unit(q_ref[a])).astype(jnp.bfloat16)

    @pl.when(pl.program_id(0) == 0)
    def _():
        z, y, c, x = place()
        owner = own_ref[...]
        local = loc_ref[...]
        oz, oy, oc = owner // (NY * 2), (owner // 2) % NY, owner % 2
        lane = lax.broadcasted_iota(jnp.int32, (REQ, 128), 1)
        row = lax.broadcasted_iota(jnp.int32, (REQ, 1), 0)
        hot = lane == (oz * 2 + oc) * NY + oy
        table = jnp.where(hot, 1.0, 0.0).astype(jnp.bfloat16)
        first = lax.broadcasted_iota(jnp.int32, (REQ, REQ), 0)
        second = lax.broadcasted_iota(jnp.int32, (REQ, REQ), 1)
        before = jnp.where(second < first, 1.0, 0.0).astype(jnp.bfloat16)
        counts = jnp.dot(before, table, preferred_element_type=jnp.float32)
        rank = jnp.sum(jnp.where(hot, counts, 0.0), axis=1, keepdims=True).astype(jnp.int32)
        article = row // NC
        held = article % NX
        spot = ((x - held + NX) % NX) * PART + article // NX
        value = jnp.where(lane < 64, spot, local)
        entry = jnp.where(lane % 64 == rank, value, 0).astype(jnp.float32).astype(jnp.bfloat16)
        lists = lax.dot_general(
            table, entry, (((0,), (0,)), ((), ())), preferred_element_type=jnp.float32
        )
        lists = lists[: WORKERS * NY].astype(jnp.int32)
        for w in range(WORKERS):
            list_ref[w, 0:NY] = lists[w * NY : (w + 1) * NY]
            list_ref[w, NY:8] = jnp.zeros((8 - NY, 128), jnp.int32)
        pos = oy * CAP + rank
        side = ((z - oz + NZ) % NZ) * 2 + jnp.where(oc == c, 0, 1)
        slot_ref[...] = jnp.where(lane < 64, side * 8 + pos % 8, pos // 8)


def prepare(owners, locals_, queries, companies):
    steps = NX
    blocks = C_DEV // steps
    return pl.pallas_call(
        prepare_kernel,
        grid=(steps,),
        out_shape=(
            jax.ShapeDtypeStruct((ARTS, E, LQ), jnp.bfloat16),
            jax.ShapeDtypeStruct((C_DEV, LC, E), jnp.bfloat16),
            jax.ShapeDtypeStruct((WORKERS, 8, 128), jnp.int32),
            jax.ShapeDtypeStruct((REQ, 128), jnp.int32),
        ),
        in_specs=[
            pl.BlockSpec((REQ, 1), lambda i: (0, 0)),
            pl.BlockSpec((REQ, 1), lambda i: (0, 0)),
            pl.BlockSpec((PART, LQ, E), lambda i: (i, 0, 0)),
            pl.BlockSpec((blocks, LC, E), lambda i: (i, 0, 0)),
        ],
        out_specs=(
            pl.BlockSpec((PART, E, LQ), lambda i: (i, 0, 0)),
            pl.BlockSpec((blocks, LC, E), lambda i: (i, 0, 0)),
            pl.BlockSpec((WORKERS, 8, 128), lambda i: (0, 0, 0)),
            pl.BlockSpec((REQ, 128), lambda i: (0, 0)),
        ),
    )(owners, locals_, queries, companies)


N_COPIES = 96


def spread_kernel(qt_ref, cat_ref, list_ref, qall_ref, slab_ref, lrecv_ref, send_sem, recv_sem, local_sem):
    z, y, c, x = place()

    def at(dz=0, dy=0, dc=0, dx=0):
        zz, yy, cc, xx = (z + dz + NZ) % NZ, (y + dy + NY) % NY, (c + dc) % 2, (x + dx + NX) % NX
        return ((zz * NY + yy) * 2 + cc, xx)

    peers = [at(dz=-d, dc=k) for d in range(NZ) for k in range(2) if d or k]
    peers += [at(dy=1), at(dy=-1), at(dx=1), at(dx=2), at(dx=3)]
    barrier = pltpu.get_barrier_semaphore()
    for peer in peers:
        pl.semaphore_signal(barrier, inc=1, device_id=peer, device_id_type=MESH)
    pl.semaphore_wait(barrier, len(peers))

    copies = {}

    def send(name, src, dst, device):
        assert name not in copies
        n = len(copies)
        copy = pltpu.make_async_remote_copy(
            src_ref=src,
            dst_ref=dst,
            send_sem=send_sem.at[n],
            recv_sem=recv_sem.at[n],
            device_id=device,
            device_id_type=MESH,
        )
        copies[name] = copy
        copy.start()

    received = set()

    def got(*names):
        for name in names:
            if name not in received:
                received.add(name)
                copies[name].wait_recv()

    own_list = pltpu.make_async_copy(list_ref.at[z * 2 + c], lrecv_ref.at[0], local_sem.at[0])
    own_list.start()
    for d in range(NZ):
        for k in range(2):
            if d or k:
                worker = ((z - d + NZ) % NZ) * 2 + (c + k) % 2
                send(f"l{d}{k}", list_ref.at[worker], lrecv_ref.at[d * 2 + k], at(dz=-d, dc=k))

    own_part = pltpu.make_async_copy(
        qt_ref.at[pl.ds(x * PART, PART)], qall_ref.at[0, 0, pl.ds(0, PART)], local_sem.at[1]
    )
    own_part.start()
    for j in (1, 3, 2):
        send(
            f"e{j}",
            qt_ref.at[pl.ds(((x + j) % NX) * PART, PART)],
            qall_ref.at[0, 0, pl.ds(j * PART, PART)],
            at(dx=j),
        )

    def z_first(j):
        rows = pl.ds(j * PART, PART)
        src = qt_ref.at[pl.ds(x * PART, PART)] if j == 0 else qall_ref.at[0, 0, rows]
        send(f"p1{j}", src, qall_ref.at[NZ - 1, 0, rows], at(dz=1))
        send(f"m1{j}", src, qall_ref.at[1, 0, rows], at(dz=-1))

    def z_next(step, half, both=(True, True)):
        rows = pl.ds(half * 2 * PART, 2 * PART)
        if both[0]:
            send(f"p{step}{half}", qall_ref.at[NZ - step + 1, 0, rows], qall_ref.at[NZ - step, 0, rows], at(dz=1))
        if both[1]:
            send(f"m{step}{half}", qall_ref.at[step - 1, 0, rows], qall_ref.at[step, 0, rows], at(dz=-1))

    def partner(dz):
        send(f"c{dz}", qall_ref.at[dz, 0], qall_ref.at[dz, 1], at(dc=1))

    def quarter(of, h):
        return pl.ds(((x + of + NX) % NX) * QUARTER + h * HALF, HALF)

    def rest(h):
        return pl.ds(SPLIT + h * REST, REST)

    def y_own(tag, rows, h):
        def up():
            send(f"up{tag}{h}", cat_ref.at[rows(h)], slab_ref.at[2, rows(h)], at(dy=1))

        def down():
            send(f"dn{tag}{h}", cat_ref.at[rows(h)], slab_ref.at[0, rows(h)], at(dy=-1))

        return up, down

    def y_fwd(tag, rows):
        send(f"up2{tag}", slab_ref.at[2, rows(0)], slab_ref.at[1, rows(0)], at(dy=1))
        send(f"dn2{tag}", slab_ref.at[0, rows(1)], slab_ref.at[1, rows(1)], at(dy=-1))

    def x_own(d, h):
        rows = quarter(0, h)
        send(f"xp{d}{h}", slab_ref.at[d, rows], slab_ref.at[d, rows], at(dx=1))
        send(f"xm{d}{h}", slab_ref.at[d, rows], slab_ref.at[d, rows], at(dx=-1))

    def x_fwd(d):
        got(f"xp{d}0")
        rows = quarter(-1, 0)
        send(f"xpf{d}", slab_ref.at[d, rows], slab_ref.at[d, rows], at(dx=1))
        got(f"xm{d}1")
        rows = quarter(1, 1)
        send(f"xmf{d}", slab_ref.at[d, rows], slab_ref.at[d, rows], at(dx=-1))

    mine = lambda h: quarter(0, h)
    y_own("s", mine, 0)[0]()
    y_own("s", mine, 1)[1]()
    y_own("s", mine, 1)[0]()
    y_own("s", mine, 0)[1]()
    z_first(0)
    got("e1")
    z_first(1)
    got("e3")
    z_first(3)
    got("ups0", "dns1")
    y_fwd("s", mine)
    for h in (0, 1):
        y_own("r", rest, h)[0]()
        y_own("r", rest, 1 - h)[1]()
    x_own(2, 0)
    x_own(0, 1)
    got("e2")
    z_first(2)
    own_part.wait()
    partner(0)
    got("p10", "p11", "m10", "m11")
    z_next(2, 0)
    got("ups1", "dns0")
    x_own(2, 1)
    x_own(0, 0)
    got("p12", "p13", "m12", "m13")
    z_next(2, 1)
    partner(NZ - 1)
    partner(1)
    got("up2s", "dn2s")
    x_own(1, 0)
    x_own(1, 1)
    got("p20", "m20")
    z_next(3, 0)
    x_fwd(2)
    x_fwd(0)
    got("p21", "m21")
    z_next(3, 1)
    partner(NZ - 2)
    partner(2)
    got("upr0", "dnr1")
    y_fwd("r", rest)
    got("p30")
    z_next(4, 0, (True, False))
    got("m30", "m31")
    z_next(4, 1, (False, True))
    got("p31")
    partner(NZ - 3)
    partner(3)
    x_fwd(1)
    got("p40", "m41")
    partner(4)
    own_list.wait()
    for name in list(copies):
        got(name)
    for copy in copies.values():
        copy.wait_send()


def spread(qt, cat, lists):
    return pl.pallas_call(
        spread_kernel,
        out_shape=(
            jax.ShapeDtypeStruct((NZ, 2, ARTS, E, LQ), jnp.bfloat16),
            jax.ShapeDtypeStruct((NY - 1, C_DEV, LC, E), jnp.bfloat16),
            jax.ShapeDtypeStruct((WORKERS, 8, 128), jnp.int32),
        ),
        in_specs=[HBM, HBM, HBM],
        out_specs=(HBM, HBM, HBM),
        scratch_shapes=[
            pltpu.SemaphoreType.DMA((N_COPIES,)),
            pltpu.SemaphoreType.DMA((N_COPIES,)),
            pltpu.SemaphoreType.DMA((2,)),
        ],
        compiler_params=pltpu.CompilerParams(collective_id=0, has_side_effects=True),
    )(qt, cat, lists)


def pool_kernel(list_ref, q_hbm, own_hbm, slab_hbm, out_ref, q_ref, cat_ref, q_sem, c_sem):
    z, y, c, x = place()
    loads = [pltpu.make_async_copy(own_hbm, cat_ref.at[y], c_sem.at[0])]
    for d in range(1, NY):
        loads.append(pltpu.make_async_copy(slab_hbm.at[d - 1], cat_ref.at[(y + d) % NY], c_sem.at[d]))

    def q_load(w):
        return pltpu.make_async_copy(q_hbm.at[w // 2, w % 2], q_ref.at[w], q_sem.at[w])

    q_load(0).start()
    for load in loads:
        load.start()
    for w in range(1, WORKERS):
        q_load(w).start()
    for load in loads:
        load.wait()
    lane = lax.broadcasted_iota(jnp.int32, (8, 128), 1)

    def source(w, carry):
        q_load(w).wait()
        scores = jnp.zeros((8, 128), jnp.float32)
        for g in range(GROUPS):
            rows = []
            for u in range(8):
                owner, slot = divmod(g * 8 + u, CAP)
                query = q_ref[w, list_ref[w, owner, slot]]
                block = cat_ref[owner, list_ref[w, owner, 64 + slot]]
                sims = jnp.dot(block, query, preferred_element_type=jnp.float32)
                mass = jnp.exp2(sims * (SHARP * math.log2(math.e)))
                rows.append(jnp.sum(jnp.sum(mass.reshape(8, 8, LQ), axis=0), axis=0, keepdims=True))
            logs = jnp.log(jnp.concatenate(rows, axis=0))
            scores = jnp.where(lane == g, jnp.sum(logs, axis=1, keepdims=True) * (1.0 / SHARP), scores)
        out_ref[w] = scores
        return carry

    lax.fori_loop(0, WORKERS, source, 0)


def pool(lists, qall, cat, slab):
    return pl.pallas_call(
        pool_kernel,
        out_shape=jax.ShapeDtypeStruct((WORKERS, 8, 128), jnp.float32),
        in_specs=[pl.BlockSpec(memory_space=pltpu.SMEM), HBM, HBM, HBM],
        out_specs=VMEM,
        scratch_shapes=[
            pltpu.VMEM((WORKERS, ARTS, E, LQ), jnp.bfloat16),
            pltpu.VMEM((NY, C_DEV, LC, E), jnp.bfloat16),
            pltpu.SemaphoreType.DMA((WORKERS,)),
            pltpu.SemaphoreType.DMA((NY,)),
        ],
        compiler_params=pltpu.CompilerParams(vmem_limit_bytes=56 << 20),
    )(lists, qall, cat, slab)


def finish_kernel(part_ref, slot_ref, rel_ref, prob_ref, recv_ref, send_sem, recv_sem, local_sem):
    z, y, c, x = place()

    def at(dz, dc):
        return ((((z + dz + NZ) % NZ) * NY + y) * 2 + (c + dc) % 2, x)

    pairs = [(d, k) for d in range(NZ) for k in range(2) if d or k]
    barrier = pltpu.get_barrier_semaphore()
    for d, k in pairs:
        pl.semaphore_signal(barrier, inc=1, device_id=at(d, k), device_id_type=MESH)
    pl.semaphore_wait(barrier, len(pairs))
    own = pltpu.make_async_copy(part_ref.at[0], recv_ref.at[0], local_sem)
    own.start()
    copies = []
    for d, k in pairs:
        n = d * 2 + k
        copies.append(
            pltpu.make_async_remote_copy(
                src_ref=part_ref.at[n],
                dst_ref=recv_ref.at[n],
                send_sem=send_sem.at[n],
                recv_sem=recv_sem.at[n],
                device_id=at(d, k),
                device_id_type=MESH,
            )
        )
        copies[-1].start()
    lane = lax.broadcasted_iota(jnp.int32, (REQ, 128), 1)
    slots = slot_ref[...]
    hot_row = jnp.where(lane == slots[:, 0:1], 1.0, 0.0).astype(jnp.bfloat16)
    hot_lane = lane == slots[:, 64:65]
    own.wait()
    for copy in copies:
        copy.wait()
    values = recv_ref[...].reshape(128, 128)
    picked = jnp.zeros((REQ, 128), jnp.float32)
    for _ in range(3):
        head = values.astype(jnp.bfloat16)
        picked = picked + jnp.dot(hot_row, head, preferred_element_type=jnp.float32)
        values = values - head.astype(jnp.float32)
    score = jnp.sum(jnp.where(hot_lane, picked, 0.0), axis=1, keepdims=True)
    wide = lax.broadcasted_iota(jnp.int32, (NC, 128), 1)
    columns = jnp.zeros((NC, 128), jnp.float32)
    for a in range(ARTS):
        columns = jnp.where(wide == a, score[a * NC : (a + 1) * NC], columns)
    relevance = columns - jnp.sum(columns, axis=0, keepdims=True) * (1.0 / NC)
    weights = jnp.exp(TEMPER * relevance)
    probs = weights / jnp.sum(weights, axis=0, keepdims=True)
    both = jnp.transpose(jnp.concatenate([relevance, probs], axis=0))
    rel_ref[...] = both[0:ARTS, 0:NC]
    prob_ref[...] = both[0:ARTS, NC:]


def finish(part, slots):
    return pl.pallas_call(
        finish_kernel,
        out_shape=(jax.ShapeDtypeStruct((ARTS, NC), jnp.float32),) * 2,
        in_specs=[HBM, VMEM],
        out_specs=(VMEM, VMEM),
        scratch_shapes=[
            pltpu.VMEM((WORKERS, 8, 128), jnp.float32),
            pltpu.SemaphoreType.DMA((WORKERS,)),
            pltpu.SemaphoreType.DMA((WORKERS,)),
            pltpu.SemaphoreType.DMA,
        ],
        compiler_params=pltpu.CompilerParams(collective_id=1, has_side_effects=True),
    )(part, slots)


def per_device(queries, cand_owner, cand_local, companies):
    held = queries.reshape(ARTS, LQ, E)
    qt, cat, lists, slots = prepare(
        cand_owner.reshape(REQ, 1), cand_local.reshape(REQ, 1), held, companies
    )
    qall, slab, mine = spread(qt, cat, lists)
    part = pool(mine, qall, cat, slab)
    return finish(part, slots)


def solution(mesh):
    placed = (
        P("art", "seq", None, None),
        P(("art", "seq"), None, None),
        P(("art", "seq"), None, None),
        P("art", None, None),
    )
    return jax.shard_map(
        per_device,
        mesh=mesh,
        in_specs=placed,
        out_specs=(P(("art", "seq"), None), P(("art", "seq"), None)),
        check_vma=False,
    )
```

time: 667 us -> 146 us (0.22); the launches traced: 657 us -> 145 us
  waiting for transfers between devices: 416 us -> 0 us
  Pallas kernels: 0 us -> 138 us
  local copies, waits for them, and re-layouts: 138 us -> 6.15 us
  other arithmetic: 42.7 us -> 0 us
  matrix products: 36.4 us -> 0 us
  starting transfers between devices: 23.8 us -> 0 us
    all_to_all x3 -> x0, waiting for transfers between devices: 416 us -> none  [the longest x1 411 us: per_device(): lax.all_to_all(catalog[lax.all_to_all(table, 'art', split_axis=0, concat_...]
    pallas_call x0 -> x4, Pallas kernels: none -> 138 us  [the longest x1 87 us: spread(): pl.pallas_call(spread_kernel, out_shape=(jax.ShapeDtypeStruct((NZ, 2, ART...]
    exp x6 -> x0, local copies, waits for them, and re-layouts: 53.5 us -> none  [pool_pair(): jnp.exp(sims * SHARP).reshape(count, tokens, NC, LC)]
    gather x2 -> x0, local copies, waits for them, and re-layouts: 43.4 us -> none  [the longest x1 28.4 us: per_device(): catalog[lax.all_to_all(table, 'art', split_axis=0, concat_axis=0, tiled=T...]
    scatter x1 -> x0, local copies, waits for them, and re-layouts: 37.5 us -> none  [per_device(): jnp.zeros((owner_count, cap_slots), jnp.int32).at[owners, slot_index]]
    dot_general x6 -> x0, matrix products: 36.4 us -> none  [pool_pair(): jnp.einsum('aqe,ake->aqk', query_pair, block_pair, preferred_element_type...]
    reduce_sum x17 -> x0, other arithmetic: 33.7 us -> none  [the longest x6 27.7 us: pool_pair(): jnp.sum(jnp.exp(sims * SHARP).reshape(count, tokens, NC, LC), axis=-1)]
    all_to_all x3 -> x0, starting transfers between devices: 23.8 us -> none  [the longest x1 13.2 us: per_device(): lax.all_to_all(table, 'art', split_axis=0, concat_axis=0, tiled=True)]
  transfers between devices with their start and end apart: 3 -> 0, of which waited for: 2 -> 0; matrix products, arithmetic and copies ran while one was open for 6% -> 0% of each run, Pallas kernels for 0% -> 0%
where the time goes in v1:
time: 146 us; the launch traced here: 145 us
  Pallas kernels  138 us (95%)
  local copies, waits for them, and re-layouts  6.15 us (4%)
    pallas_call x1, Pallas kernels, spread(): pl.pallas_call(spread_kernel, out_shape=(jax.ShapeDtypeStruct((NZ, 2, ART...  87 us
    pallas_call x1, Pallas kernels, pool(): pl.pallas_call(pool_kernel, out_shape=jax.ShapeDtypeStruct((WORKERS, 8, 1...  27.2 us
    pallas_call x1, Pallas kernels, finish(): pl.pallas_call(finish_kernel, out_shape=(jax.ShapeDtypeStruct((ARTS, NC),...  12.7 us
    pallas_call x1, Pallas kernels, prepare(): pl.pallas_call(prepare_kernel, grid=(steps,), out_shape=(jax.ShapeDtypeSt...  11.5 us
    unnamed x4, local copies, waits for them, and re-layouts  4.35 us

profile of v1, /device:TPU:1, one launch (start us, length us, event | category | flops | bytes accessed | tf_op | source)
XLA Modules:
  0.0 145.2 jit_solution(9454985197375962428)
XLA Ops:
  0.6 0.9 copy.8
  1.5 0.9 copy.9
  2.4 0.9 reshape.17.loc_ref
  3.3 0.9 reshape.16.own_ref
  4.2 11.5 %shard_map.59 = (bf16[12,128,256]{2,1,0:T(8,128)(2,1)}, bf16[256,64,128]{2,1,0:T(8,128)(2,1)}, s32[16,8,128]{2,1,0:T(8,128)}, s32[768,128]{1,0:T(8,128)}) custom-call(s32[768,1]{1,0:T(8,128)} %reshape.16.own_ref, s32[768,1]{1,0:T(8,128)} %reshape.17.loc_ref, bf16[12,256,128]{2,1,0:T(8,128)(2,1)} %bitcast.1, bf16[256,64,128]{2,1,0:T(8,128)(2,1)} %c_ref.1), custom_call_target="tpu_custom_call" | custom-call | tf_op jit(solution)/shard_map/pallas_call | solution.py:88
  15.7 87.0 %shard_map.60 = (bf16[8,2,12,128,256]{4,3,2,1,0:T(8,128)(2,1)}, bf16[3,256,64,128]{3,2,1,0:T(8,128)(2,1)}, s32[16,8,128]{2,1,0:T(8,128)}) custom-call(bf16[12,128,256]{2,1,0:T(8,128)(2,1)} %get-tuple-element.9.qt_ref, bf16[256,64,128]{2,1,0:T(8,128)(2,1)} %get-tuple-element.10.cat_ref.own_hbm, s32[16,8,128]{2,1,0:T(8,128)} %get-tuple-element.11.list_ref), custom_call_target="tpu_custom_call" | custom-call | tf_op jit(solution)/shard_map/pallas_call | solution.py:282
  102.7 27.2 %shard_map.61.part_ref = f32[16,8,128]{2,1,0:T(8,128)} custom-call(s32[16,8,128]{2,1,0:T(8,128)} %get-tuple-element.12.list_ref, bf16[8,2,12,128,256]{4,3,2,1,0:T(8,128)(2,1)} %get-tuple-element.13.q_hbm, bf16[256,64,128]{2,1,0:T(8,128)(2,1)} %get-tuple-element.10.cat_ref.own_hbm, bf16[3,256,64,128]{3,2,1,0:T(8,128)(2,1)} %get-tuple-element.14.slab_hbm), custom_call_target="tpu_custom_call" | custom-call | tf_op jit(solution)/shard_map/pallas_call | solution.py:339
  129.9 12.7 %shard_map.62 = (f32[12,64]{1,0:T(8,128)}, f32[12,64]{1,0:T(8,128)}) custom-call(f32[16,8,128]{2,1,0:T(8,128)} %shard_map.61.part_ref, s32[768,128]{1,0:T(8,128)} %get-tuple-element.15.slot_ref), custom_call_target="tpu_custom_call" | custom-call | tf_op jit(solution)/shard_map/pallas_call | solution.py:408
  142.6 1.3 copy.14
  143.9 1.3 copy.15

commit v2 on v1

--- a/solution.py
+++ b/solution.py
@@ -21,8 +21,8 @@
 NC = 64
 C_DEV = 256
 CAP = 18
-SLOTS = NY * CAP
-GROUPS = SLOTS // 8
+GROUP = 6
+GROUPS = CAP // GROUP
 WORKERS = NZ * 2
 REQ = ARTS * NC
 SPLIT = 160
@@ -77,9 +77,9 @@
         for w in range(WORKERS):
             list_ref[w, 0:NY] = lists[w * NY : (w + 1) * NY]
             list_ref[w, NY:8] = jnp.zeros((8 - NY, 128), jnp.int32)
-        pos = oy * CAP + rank
         side = ((z - oz + NZ) % NZ) * 2 + jnp.where(oc == c, 0, 1)
-        slot_ref[...] = jnp.where(lane < 64, side * 8 + pos % 8, pos // 8)
+        column = ((oy - y + NY) % NY) * GROUPS + rank // GROUP
+        slot_ref[...] = jnp.where(lane < 64, side * 8 + rank % GROUP, column)
 
 
 def prepare(owners, locals_, queries, companies):
@@ -109,10 +109,14 @@
     )(owners, locals_, queries, companies)
 
 
-N_COPIES = 96
-
-
-def spread_kernel(qt_ref, cat_ref, list_ref, qall_ref, slab_ref, lrecv_ref, send_sem, recv_sem, local_sem):
+N_COPIES = 100
+
+
+def meet_kernel(
+    qt_ref, cat_ref, list_ref, back_ref,
+    qall_ref, cat0, cat1, cat2, cat3, lrecv_ref, lists, part_ref, send_sem, recv_sem, local_sem,
+):
+    slabs = (cat1, cat2, cat3)
     z, y, c, x = place()
 
     def at(dz=0, dy=0, dc=0, dx=0):
@@ -158,6 +162,10 @@
                 worker = ((z - d + NZ) % NZ) * 2 + (c + k) % 2
                 send(f"l{d}{k}", list_ref.at[worker], lrecv_ref.at[d * 2 + k], at(dz=-d, dc=k))
 
+    own_cat = pltpu.make_async_copy(cat_ref, cat0, local_sem.at[2])
+    own_cat.start()
+    lane = lax.broadcasted_iota(jnp.int32, (8, 128), 1)
+
     own_part = pltpu.make_async_copy(
         qt_ref.at[pl.ds(x * PART, PART)], qall_ref.at[0, 0, pl.ds(0, PART)], local_sem.at[1]
     )
@@ -194,29 +202,29 @@
 
     def y_own(tag, rows, h):
         def up():
-            send(f"up{tag}{h}", cat_ref.at[rows(h)], slab_ref.at[2, rows(h)], at(dy=1))
+            send(f"up{tag}{h}", cat_ref.at[rows(h)], slabs[2].at[rows(h)], at(dy=1))
 
         def down():
-            send(f"dn{tag}{h}", cat_ref.at[rows(h)], slab_ref.at[0, rows(h)], at(dy=-1))
+            send(f"dn{tag}{h}", cat_ref.at[rows(h)], slabs[0].at[rows(h)], at(dy=-1))
 
         return up, down
 
     def y_fwd(tag, rows):
-        send(f"up2{tag}", slab_ref.at[2, rows(0)], slab_ref.at[1, rows(0)], at(dy=1))
-        send(f"dn2{tag}", slab_ref.at[0, rows(1)], slab_ref.at[1, rows(1)], at(dy=-1))
+        send(f"up2{tag}", slabs[2].at[rows(0)], slabs[1].at[rows(0)], at(dy=1))
+        send(f"dn2{tag}", slabs[0].at[rows(1)], slabs[1].at[rows(1)], at(dy=-1))
 
     def x_own(d, h):
         rows = quarter(0, h)
-        send(f"xp{d}{h}", slab_ref.at[d, rows], slab_ref.at[d, rows], at(dx=1))
-        send(f"xm{d}{h}", slab_ref.at[d, rows], slab_ref.at[d, rows], at(dx=-1))
+        send(f"xp{d}{h}", slabs[d].at[rows], slabs[d].at[rows], at(dx=1))
+        send(f"xm{d}{h}", slabs[d].at[rows], slabs[d].at[rows], at(dx=-1))
 
     def x_fwd(d):
         got(f"xp{d}0")
         rows = quarter(-1, 0)
-        send(f"xpf{d}", slab_ref.at[d, rows], slab_ref.at[d, rows], at(dx=1))
+        send(f"xpf{d}", slabs[d].at[rows], slabs[d].at[rows], at(dx=1))
         got(f"xm{d}1")
         rows = quarter(1, 1)
-        send(f"xmf{d}", slab_ref.at[d, rows], slab_ref.at[d, rows], at(dx=-1))
+        send(f"xmf{d}", slabs[d].at[rows], slabs[d].at[rows], at(dx=-1))
 
     mine = lambda h: quarter(0, h)
     y_own("s", mine, 0)[0]()
@@ -237,6 +245,10 @@
     x_own(0, 1)
     got("e2")
     z_first(2)
+    own_list.wait()
+    got(*[n for n in copies if n[0] == "l"])
+    list_copy = pltpu.make_async_copy(lrecv_ref, lists, local_sem.at[3])
+    list_copy.start()
     own_part.wait()
     partner(0)
     got("p10", "p11", "m10", "m11")
@@ -271,120 +283,84 @@
     x_fwd(1)
     got("p40", "m41")
     partner(4)
-    own_list.wait()
+    got(*[n for n in copies if n[0] in "epmc"])
+
+    def score(d):
+        cat = (cat0, cat1, cat2, cat3)[d]
+        owner = (y + d) % NY
+
+        def tile(dz, carry):
+            for k in range(2):
+                w = dz * 2 + k
+                scores = jnp.zeros((8, 128), jnp.float32) if d == 0 else part_ref[w]
+                for g in range(GROUPS):
+                    rows = []
+                    for u in range(GROUP):
+                        slot = g * GROUP + u
+                        query = qall_ref[dz, k, lists[w, owner, slot]]
+                        block = cat[lists[w, owner, 64 + slot]]
+                        sims = jnp.dot(block, query, preferred_element_type=jnp.float32)
+                        mass = jnp.exp2(sims * (SHARP * math.log2(math.e)))
+                        rows.append(jnp.sum(jnp.sum(mass.reshape(8, 8, LQ), axis=0), axis=0, keepdims=True))
+                    rows += [jnp.ones((8 - GROUP, LQ), jnp.float32)]
+                    logs = jnp.log(jnp.concatenate(rows, axis=0))
+                    total = jnp.sum(logs, axis=1, keepdims=True) * (1.0 / SHARP)
+                    scores = jnp.where(lane == d * GROUPS + g, total, scores)
+                part_ref[w] = scores
+            return carry
+
+        lax.fori_loop(0, NZ, tile, 0)
+
+    own_cat.wait()
+    list_copy.wait()
+    score(0)
+    got("dns0", "dns1", "dnr0", "dnr1", "xp00", "xp01", "xm00", "xm01", "xpf0", "xmf0")
+    score(1)
+    got("ups0", "ups1", "upr0", "upr1", "xp20", "xp21", "xm20", "xm21", "xpf2", "xmf2")
+    score(3)
+    for name in list(copies):
+        got(name)
+    score(2)
+    own_part = pltpu.make_async_copy(part_ref.at[0], back_ref.at[0], local_sem.at[0])
+    own_part.start()
+    for d in range(NZ):
+        for k in range(2):
+            if d or k:
+                send(f"b{d}{k}", part_ref.at[d * 2 + k], back_ref.at[d * 2 + k], at(dz=d, dc=k))
+    own_part.wait()
     for name in list(copies):
         got(name)
     for copy in copies.values():
         copy.wait_send()
 
 
-def spread(qt, cat, lists):
+def meet(qt, cat, lists):
     return pl.pallas_call(
-        spread_kernel,
-        out_shape=(
-            jax.ShapeDtypeStruct((NZ, 2, ARTS, E, LQ), jnp.bfloat16),
-            jax.ShapeDtypeStruct((NY - 1, C_DEV, LC, E), jnp.bfloat16),
-            jax.ShapeDtypeStruct((WORKERS, 8, 128), jnp.int32),
-        ),
+        meet_kernel,
+        out_shape=jax.ShapeDtypeStruct((WORKERS, 8, 128), jnp.float32),
         in_specs=[HBM, HBM, HBM],
-        out_specs=(HBM, HBM, HBM),
-        scratch_shapes=[
+        out_specs=VMEM,
+        scratch_shapes=[pltpu.VMEM((NZ, 2, ARTS, E, LQ), jnp.bfloat16)]
+        + [pltpu.VMEM((C_DEV, LC, E), jnp.bfloat16)] * NY
+        + [
+            pltpu.VMEM((WORKERS, 8, 128), jnp.int32),
+            pltpu.SMEM((WORKERS, 8, 128), jnp.int32),
+            pltpu.VMEM((WORKERS, 8, 128), jnp.float32),
             pltpu.SemaphoreType.DMA((N_COPIES,)),
             pltpu.SemaphoreType.DMA((N_COPIES,)),
-            pltpu.SemaphoreType.DMA((2,)),
+            pltpu.SemaphoreType.DMA((4,)),
         ],
-        compiler_params=pltpu.CompilerParams(collective_id=0, has_side_effects=True),
+        compiler_params=pltpu.CompilerParams(
+            collective_id=0, has_side_effects=True, vmem_limit_bytes=48 << 20
+        ),
     )(qt, cat, lists)
 
 
-def pool_kernel(list_ref, q_hbm, own_hbm, slab_hbm, out_ref, q_ref, cat_ref, q_sem, c_sem):
-    z, y, c, x = place()
-    loads = [pltpu.make_async_copy(own_hbm, cat_ref.at[y], c_sem.at[0])]
-    for d in range(1, NY):
-        loads.append(pltpu.make_async_copy(slab_hbm.at[d - 1], cat_ref.at[(y + d) % NY], c_sem.at[d]))
-
-    def q_load(w):
-        return pltpu.make_async_copy(q_hbm.at[w // 2, w % 2], q_ref.at[w], q_sem.at[w])
-
-    q_load(0).start()
-    for load in loads:
-        load.start()
-    for w in range(1, WORKERS):
-        q_load(w).start()
-    for load in loads:
-        load.wait()
-    lane = lax.broadcasted_iota(jnp.int32, (8, 128), 1)
-
-    def source(w, carry):
-        q_load(w).wait()
-        scores = jnp.zeros((8, 128), jnp.float32)
-        for g in range(GROUPS):
-            rows = []
-            for u in range(8):
-                owner, slot = divmod(g * 8 + u, CAP)
-                query = q_ref[w, list_ref[w, owner, slot]]
-                block = cat_ref[owner, list_ref[w, owner, 64 + slot]]
-                sims = jnp.dot(block, query, preferred_element_type=jnp.float32)
-                mass = jnp.exp2(sims * (SHARP * math.log2(math.e)))
-                rows.append(jnp.sum(jnp.sum(mass.reshape(8, 8, LQ), axis=0), axis=0, keepdims=True))
-            logs = jnp.log(jnp.concatenate(rows, axis=0))
-            scores = jnp.where(lane == g, jnp.sum(logs, axis=1, keepdims=True) * (1.0 / SHARP), scores)
-        out_ref[w] = scores
-        return carry
-
-    lax.fori_loop(0, WORKERS, source, 0)
-
-
-def pool(lists, qall, cat, slab):
-    return pl.pallas_call(
-        pool_kernel,
-        out_shape=jax.ShapeDtypeStruct((WORKERS, 8, 128), jnp.float32),
-        in_specs=[pl.BlockSpec(memory_space=pltpu.SMEM), HBM, HBM, HBM],
-        out_specs=VMEM,
-        scratch_shapes=[
-            pltpu.VMEM((WORKERS, ARTS, E, LQ), jnp.bfloat16),
-            pltpu.VMEM((NY, C_DEV, LC, E), jnp.bfloat16),
-            pltpu.SemaphoreType.DMA((WORKERS,)),
-            pltpu.SemaphoreType.DMA((NY,)),
-        ],
-        compiler_params=pltpu.CompilerParams(vmem_limit_bytes=56 << 20),
-    )(lists, qall, cat, slab)
-
-
-def finish_kernel(part_ref, slot_ref, rel_ref, prob_ref, recv_ref, send_sem, recv_sem, local_sem):
-    z, y, c, x = place()
-
-    def at(dz, dc):
-        return ((((z + dz + NZ) % NZ) * NY + y) * 2 + (c + dc) % 2, x)
-
-    pairs = [(d, k) for d in range(NZ) for k in range(2) if d or k]
-    barrier = pltpu.get_barrier_semaphore()
-    for d, k in pairs:
-        pl.semaphore_signal(barrier, inc=1, device_id=at(d, k), device_id_type=MESH)
-    pl.semaphore_wait(barrier, len(pairs))
-    own = pltpu.make_async_copy(part_ref.at[0], recv_ref.at[0], local_sem)
-    own.start()
-    copies = []
-    for d, k in pairs:
-        n = d * 2 + k
-        copies.append(
-            pltpu.make_async_remote_copy(
-                src_ref=part_ref.at[n],
-                dst_ref=recv_ref.at[n],
-                send_sem=send_sem.at[n],
-                recv_sem=recv_sem.at[n],
-                device_id=at(d, k),
-                device_id_type=MESH,
-            )
-        )
-        copies[-1].start()
+def finish_kernel(recv_ref, slot_ref, rel_ref, prob_ref):
     lane = lax.broadcasted_iota(jnp.int32, (REQ, 128), 1)
     slots = slot_ref[...]
     hot_row = jnp.where(lane == slots[:, 0:1], 1.0, 0.0).astype(jnp.bfloat16)
     hot_lane = lane == slots[:, 64:65]
-    own.wait()
-    for copy in copies:
-        copy.wait()
     values = recv_ref[...].reshape(128, 128)
     picked = jnp.zeros((REQ, 128), jnp.float32)
     for _ in range(3):
@@ -408,15 +384,8 @@
     return pl.pallas_call(
         finish_kernel,
         out_shape=(jax.ShapeDtypeStruct((ARTS, NC), jnp.float32),) * 2,
-        in_specs=[HBM, VMEM],
+        in_specs=[VMEM, VMEM],
         out_specs=(VMEM, VMEM),
-        scratch_shapes=[
-            pltpu.VMEM((WORKERS, 8, 128), jnp.float32),
-            pltpu.SemaphoreType.DMA((WORKERS,)),
-            pltpu.SemaphoreType.DMA((WORKERS,)),
-            pltpu.SemaphoreType.DMA,
-        ],
-        compiler_params=pltpu.CompilerParams(collective_id=1, has_side_effects=True),
     )(part, slots)
 
 
@@ -425,9 +394,7 @@
     qt, cat, lists, slots = prepare(
         cand_owner.reshape(REQ, 1), cand_local.reshape(REQ, 1), held, companies
     )
-    qall, slab, mine = spread(qt, cat, lists)
-    part = pool(mine, qall, cat, slab)
-    return finish(part, slots)
+    return finish(meet(qt, cat, lists), slots)
 
 
 def solution(mesh):

time: 146 us -> 124 us (0.85)
  Pallas kernels: 138 us -> 115 us
  local copies, waits for them, and re-layouts: 6.15 us -> 8.35 us
    pallas_call x2 -> x1, Pallas kernels: 114 us -> 101 us  [meet(): pl.pallas_call(meet_kernel, out_shape=jax.ShapeDtypeStruct((WORKERS, 8, 1...]
    pallas_call x1, Pallas kernels: 12.7 us -> 2.25 us  [finish(): pl.pallas_call(finish_kernel, out_shape=(jax.ShapeDtypeStruct((ARTS, NC),...]
    unnamed x4 -> x10, local copies, waits for them, and re-layouts: 4.35 us -> 6.52 us
where the time goes in v2:
time: 124 us
  Pallas kernels  115 us (93%)
  local copies, waits for them, and re-layouts  8.35 us (7%)
    pallas_call x1, Pallas kernels, meet(): pl.pallas_call(meet_kernel, out_shape=jax.ShapeDtypeStruct((WORKERS, 8, 1...  101 us
    pallas_call x1, Pallas kernels, prepare(): pl.pallas_call(prepare_kernel, grid=(steps,), out_shape=(jax.ShapeDtypeSt...  11.4 us
    unnamed x10, local copies, waits for them, and re-layouts  6.52 us

profile of v2, /device:TPU:1, one launch (start us, length us, event | category | flops | bytes accessed | tf_op | source)
XLA Modules:
  0.0 123.9 jit_solution(2043995595651169410)
XLA Ops:
  0.6 0.9 copy.8
  1.5 0.9 copy.9
  2.4 0.9 reshape.17.loc_ref
  3.3 0.9 reshape.16.own_ref
  4.2 11.4 %shard_map.59 = (bf16[12,128,256]{2,1,0:T(8,128)(2,1)}, bf16[256,64,128]{2,1,0:T(8,128)(2,1)}, s32[16,8,128]{2,1,0:T(8,128)}, s32[768,128]{1,0:T(8,128)}) custom-call(s32[768,1]{1,0:T(8,128)} %reshape.16.own_ref, s32[768,1]{1,0:T(8,128)} %reshape.17.loc_ref, bf16[12,256,128]{2,1,0:T(8,128)(2,1)} %bitcast.1, bf16[256,64,128]{2,1,0:T(8,128)(2,1)} %c_ref.1), custom_call_target="tpu_custom_call" | custom-call | tf_op jit(solution)/shard_map/pallas_call | solution.py:88
  15.6 0.0 copy-start
  15.6 2.2 %copy-done = bf16[256,64,128]{2,1,0:T(8,128)(2,1)S(1)} copy-done((bf16[256,64,128]{2,1,0:T(8,128)(2,1)S(1)}, bf16[256,64,128]{2,1,0:T(8,128)(2,1)}, u32[]{:S(2)}) %copy-start) | copy-done | bytes 4194328
  17.8 0.0 copy-start.1
  17.8 1.1 copy-done.1
  18.9 0.0 copy-start.3
  18.9 0.8 copy-done.3
  19.8 101.2 %shard_map.60.recv_ref = f32[16,8,128]{2,1,0:T(8,128)S(1)} custom-call(bf16[12,128,256]{2,1,0:T(8,128)(2,1)S(1)} %copy-done.1, bf16[256,64,128]{2,1,0:T(8,128)(2,1)S(1)} %copy-done, s32[16,8,128]{2,1,0:T(8,128)S(1)} %copy-done.3), custom_call_target="tpu_custom_call" | custom-call | tf_op jit(solution)/shard_map/pallas_call | solution.py:338
  121.0 0.0 copy-start.2
  121.0 0.6 copy-done.2
  121.6 2.2 %shard_map.61 = (f32[12,64]{1,0:T(8,128)}, f32[12,64]{1,0:T(8,128)}) custom-call(f32[16,8,128]{2,1,0:T(8,128)} %copy-done.2, s32[768,128]{1,0:T(8,128)} %get-tuple-element.9.slot_ref), custom_call_target="tpu_custom_call" | custom-call | tf_op jit(solution)/shard_map/pallas_call | solution.py:384
Async XLA Ops:
  15.6 2.2 %copy-start = (bf16[256,64,128]{2,1,0:T(8,128)(2,1)S(1)}, bf16[256,64,128]{2,1,0:T(8,128)(2,1)}, u32[]{:S(2)}) copy-start(bf16[256,64,128]{2,1,0:T(8,128)(2,1)} %get-tuple-element.7.cat_ref) | copy-start | bytes 12582916
  17.8 1.1 copy-start.1
  18.9 0.8 copy-start.3
  121.0 0.6 copy-start.2

commit v3 on v2

v3 whole, which is shorter than its diff:
```python
import math

import jax
import jax.numpy as jnp
from jax import lax
from jax.experimental import pallas as pl
from jax.experimental.pallas import tpu as pltpu
from jax.sharding import PartitionSpec as P

EPS = 1e-06
SHARP = 16.0
TEMPER = 4.0
MESH = pl.DeviceIdType.MESH
HBM = pl.BlockSpec(memory_space=pl.ANY)
VMEM = pl.BlockSpec(memory_space=pltpu.VMEM)

NX, NY, NZ = 4, 4, 8
ARTS = 12
PART = ARTS // NX
LQ, LC, E = 256, 64, 128
NC = 64
ROWS, PER = 16, 4
C_DEV = 256
CAP = 18
GROUP = 6
GROUPS = CAP // GROUP
WORKERS = NZ * 2
REQ = ARTS * NC
SPLIT = 160
QUARTER = SPLIT // NX
HALF = QUARTER // 2
REST = (C_DEV - SPLIT) // 2
RING = (0, 7, 1, 6, 2, 5, 3, 4)
SPOT = {dz: i for i, dz in enumerate(RING)}
NEAR = 5
N_COPIES = 112


def unit(values):
    wide = values.astype(jnp.float32)
    return wide * lax.rsqrt(jnp.sum(wide * wide, axis=-1, keepdims=True) + EPS)


def place():
    art, x = lax.axis_index("art"), lax.axis_index("seq")
    return art // (NY * 2), (art // 2) % NY, art % 2, x


def column(ref):
    table = ref[...].reshape(ARTS * PER, ROWS)
    return jnp.concatenate([table[:, r : r + 1] for r in range(ROWS)], axis=0)


def list_kernel(own_ref, loc_ref, list_ref, slot_ref):
    z, y, c, x = place()
    owner, local = column(own_ref), column(loc_ref)
    oz, oy, oc = owner // (NY * 2), (owner // 2) % NY, owner % 2
    lane = lax.broadcasted_iota(jnp.int32, (REQ, 128), 1)
    row = lax.broadcasted_iota(jnp.int32, (REQ, 1), 0)
    hot = lane == (oz * 2 + oc) * NY + oy
    table = jnp.where(hot, 1.0, 0.0).astype(jnp.bfloat16)
    first = lax.broadcasted_iota(jnp.int32, (REQ, REQ), 0)
    second = lax.broadcasted_iota(jnp.int32, (REQ, REQ), 1)
    before = jnp.where(second < first, 1.0, 0.0).astype(jnp.bfloat16)
    counts = jnp.dot(before, table, preferred_element_type=jnp.float32)
    rank = jnp.sum(jnp.where(hot, counts, 0.0), axis=1, keepdims=True).astype(jnp.int32)
    article = (row % (ARTS * PER)) // PER
    spot = ((x - article % NX + NX) % NX) * PART + article // NX
    value = jnp.where(lane < 64, spot, local)
    entry = jnp.where(lane % 64 == rank, value, 0).astype(jnp.float32).astype(jnp.bfloat16)
    lists = lax.dot_general(table, entry, (((0,), (0,)), ((), ())), preferred_element_type=jnp.float32)
    lists = lists[: WORKERS * NY].astype(jnp.int32)
    for w in range(WORKERS):
        list_ref[w, 0:NY] = lists[w * NY : (w + 1) * NY]
        list_ref[w, NY:8] = jnp.zeros((8 - NY, 128), jnp.int32)
    dz = (z - oz + NZ) % NZ
    ring = jnp.where(dz < NZ // 2, 2 * dz, 2 * (NZ - dz) - 1)
    side = ring * 2 + jnp.where(oc == c, 0, 1)
    spot_lane = ((oy - y + NY) % NY) * GROUPS + rank // GROUP
    slot_ref[...] = jnp.where(lane < 64, side * 8 + rank % GROUP, spot_lane)


def make_lists(owners, locals_):
    return pl.pallas_call(
        list_kernel,
        out_shape=(
            jax.ShapeDtypeStruct((WORKERS, 8, 128), jnp.int32),
            jax.ShapeDtypeStruct((REQ, 128), jnp.int32),
        ),
        in_specs=[VMEM, VMEM],
        out_specs=(VMEM, VMEM),
    )(owners, locals_)


def meet_kernel(
    list_ref, q_hbm, c_hbm, back_ref,
    raw_ref, qt_ref, near_ref, far_ref, cat0, cat1, cat2, cat3,
    lrecv_ref, lists, part_ref, send_sem, recv_sem, local_sem,
):
    slabs = (cat1, cat2, cat3)
    z, y, c, x = place()

    def at(dz=0, dy=0, dc=0, dx=0):
        zz, yy, cc, xx = (z + dz + NZ) % NZ, (y + dy + NY) % NY, (c + dc) % 2, (x + dx + NX) % NX
        return ((zz * NY + yy) * 2 + cc, xx)

    peers = [at(dz=-d, dc=k) for d in range(NZ) for k in range(2) if d or k]
    peers += [at(dy=1), at(dy=-1), at(dx=1), at(dx=2), at(dx=3)]
    barrier = pltpu.get_barrier_semaphore()
    for peer in peers:
        pl.semaphore_signal(barrier, inc=1, device_id=peer, device_id_type=MESH)

    def load(src, dst, n):
        copy = pltpu.make_async_copy(src, dst, local_sem.at[n])
        copy.start()
        return copy

    def quarter(of, h):
        return pl.ds(((x + of + NX) % NX) * QUARTER + h * HALF, HALF)

    def rest(h):
        return pl.ds(SPLIT + h * REST, REST)

    whole = [pl.ds(((x + of) % NX) * QUARTER, QUARTER) for of in range(NX)]
    tail = pl.ds(SPLIT, C_DEV - SPLIT)
    in_first = load(c_hbm.at[whole[0]], cat0.at[whole[0]], 0)
    in_query = load(q_hbm, raw_ref, 1)
    in_tail = load(c_hbm.at[tail], cat0.at[tail], 2)
    in_other = [load(c_hbm.at[whole[of]], cat0.at[whole[of]], 2 + of) for of in (1, 2, 3)]

    def normalise(start, count):
        def some(i, carry):
            rows = pl.ds(start + i * 8, 8)
            cat0[rows] = unit(cat0[rows]).astype(jnp.bfloat16)
            return carry

        lax.fori_loop(0, count // 8, some, 0)

    in_first.wait()
    normalise(x * QUARTER, QUARTER)
    in_query.wait()
    for a in range(ARTS):
        qt_ref[a] = jnp.transpose(unit(raw_ref[a])).astype(jnp.bfloat16)
    for m in range(PART):
        near_ref[0, 0, m] = qt_ref[x * PART + m]
    pl.semaphore_wait(barrier, len(peers))

    copies = {}

    def send(name, src, dst, device):
        assert name not in copies
        n = len(copies)
        copy = pltpu.make_async_remote_copy(
            src_ref=src,
            dst_ref=dst,
            send_sem=send_sem.at[n],
            recv_sem=recv_sem.at[n],
            device_id=device,
            device_id_type=MESH,
        )
        copies[name] = copy
        copy.start()

    received = set()

    def got(*names):
        for name in names:
            if name not in received:
                received.add(name)
                copies[name].wait_recv()

    def tile(dz, k):
        i = SPOT[dz]
        return near_ref.at[i, k] if i < NEAR else far_ref.at[i - NEAR, k]

    def z_first(j):
        rows = pl.ds(j * PART, PART)
        src = tile(0, 0).at[rows]
        send(f"p1{j}", src, tile(NZ - 1, 0).at[rows], at(dz=1))
        send(f"m1{j}", src, tile(1, 0).at[rows], at(dz=-1))

    def z_next(step, half, both=(True, True)):
        rows = pl.ds(half * 2 * PART, 2 * PART)
        if both[0]:
            send(f"p{step}{half}", tile(NZ - step + 1, 0).at[rows], tile(NZ - step, 0).at[rows], at(dz=1))
        if both[1]:
            send(f"m{step}{half}", tile(step - 1, 0).at[rows], tile(step, 0).at[rows], at(dz=-1))

    def partner(dz):
        send(f"c{dz}", tile(dz, 0), tile(dz, 1), at(dc=1))

    def y_up(tag, rows, h):
        send(f"up{tag}{h}", cat0.at[rows(h)], slabs[2].at[rows(h)], at(dy=1))

    def y_down(tag, rows, h):
        send(f"dn{tag}{h}", cat0.at[rows(h)], slabs[0].at[rows(h)], at(dy=-1))

    def y_fwd(tag, rows):
        send(f"upf{tag}", slabs[2].at[rows(0)], slabs[1].at[rows(0)], at(dy=1))
        send(f"dnf{tag}", slabs[0].at[rows(1)], slabs[1].at[rows(1)], at(dy=-1))

    def x_own(d, h):
        rows = quarter(0, h)
        send(f"xp{d}{h}", slabs[d].at[rows], slabs[d].at[rows], at(dx=1))
        send(f"xm{d}{h}", slabs[d].at[rows], slabs[d].at[rows], at(dx=-1))

    def x_fwd(d):
        got(f"xp{d}0")
        rows = quarter(-1, 0)
        send(f"xpf{d}", slabs[d].at[rows], slabs[d].at[rows], at(dx=1))
        got(f"xm{d}1")
        rows = quarter(1, 1)
        send(f"xmf{d}", slabs[d].at[rows], slabs[d].at[rows], at(dx=-1))

    def mine(h):
        return quarter(0, h)

    y_up("s", mine, 0)
    y_down("s", mine, 1)
    y_up("s", mine, 1)
    y_down("s", mine, 0)
    for j in (1, 3, 2):
        send(
            f"e{j}",
            qt_ref.at[pl.ds(((x + j) % NX) * PART, PART)],
            tile(0, 0).at[pl.ds(j * PART, PART)],
            at(dx=j),
        )
    z_first(0)
    in_tail.wait()
    normalise(SPLIT, C_DEV - SPLIT)
    got("e1")
    z_first(1)
    got("e3")
    z_first(3)
    got("ups0", "dns1")
    y_fwd("s", mine)
    for h in (0, 1):
        y_up("r", rest, h)
        y_down("r", rest, 1 - h)
    x_own(2, 0)
    x_own(0, 1)
    got("e2")
    z_first(2)
    partner(0)
    got("p10", "p11", "m10", "m11")
    z_next(2, 0)
    own_list = load(list_ref.at[z * 2 + c], lrecv_ref.at[0], 0)
    for d in range(NZ):
        for k in range(2):
            if d or k:
                worker = ((z - d + NZ) % NZ) * 2 + (c + k) % 2
                send(f"l{d}{k}", list_ref.at[worker], lrecv_ref.at[SPOT[d] * 2 + k], at(dz=-d, dc=k))
    got("ups1", "dns0")
    x_own(2, 1)
    x_own(0, 0)
    got("p12", "p13", "m12", "m13")
    z_next(2, 1)
    partner(NZ - 1)
    partner(1)
    got("upfs", "dnfs")
    x_own(1, 0)
    x_own(1, 1)
    own_list.wait()
    got(*[n for n in copies if n[0] == "l"])
    lists_in = load(lrecv_ref, lists, 0)
    for of in (1, 2, 3):
        in_other[of - 1].wait()
        normalise(((x + of) % NX) * QUARTER, QUARTER)
    got("p20", "m20")
    z_next(3, 0)
    x_fwd(2)
    x_fwd(0)
    got("p21", "m21")
    z_next(3, 1)
    partner(NZ - 2)
    partner(2)
    got("upr0", "dnr1")
    y_fwd("r", rest)
    lists_in.wait()

    lane = lax.broadcasted_iota(jnp.int32, (8, 128), 1)
    cats = (cat0, cat1, cat2, cat3)

    def score(d, queries, i, base):
        owner = (y + d) % NY
        for k in range(2):
            w = (base + i) * 2 + k
            scores = jnp.zeros((8, 128), jnp.float32) if d == 0 else part_ref[w]
            for g in range(GROUPS):
                rows = []
                for u in range(GROUP):
                    slot = g * GROUP + u
                    query = queries[i, k, lists[w, owner, slot]]
                    block = cats[d][lists[w, owner, 64 + slot]]
                    sims = jnp.dot(block, query, preferred_element_type=jnp.float32)
                    mass = jnp.exp2(sims * (SHARP * math.log2(math.e)))
                    rows.append(jnp.sum(jnp.sum(mass.reshape(8, 8, LQ), axis=0), axis=0, keepdims=True))
                rows += [jnp.ones((8 - GROUP, LQ), jnp.float32)]
                logs = jnp.log(jnp.concatenate(rows, axis=0))
                total = jnp.sum(logs, axis=1, keepdims=True) * (1.0 / SHARP)
                scores = jnp.where(lane == d * GROUPS + g, total, scores)
            part_ref[w] = scores

    def wave(d, far):
        queries, base, count = (far_ref, NEAR, NZ - NEAR) if far else (near_ref, 0, NEAR)

        def body(i, carry):
            score(d, queries, i, base)
            return carry

        lax.fori_loop(0, count, body, 0)

    got("c0", "c1", f"c{NZ - 1}", "c2", f"c{NZ - 2}")
    wave(0, False)
    got("p30")
    z_next(4, 0, (True, False))
    x_fwd(1)
    got("m30", "m31")
    z_next(4, 1, (False, True))
    got("p31")
    partner(NZ - 3)
    partner(3)
    got("dns0", "dns1", "dnr0", "dnr1", "xp00", "xp01", "xm00", "xm01", "xpf0", "xmf0")
    wave(1, False)
    got("p40", "m41")
    partner(4)
    got("ups0", "ups1", "upr0", "upr1", "xp20", "xp21", "xm20", "xm21", "xpf2", "xmf2")
    wave(3, False)
    got(*[n for n in copies if n[0] == "c"])
    wave(0, True)
    wave(1, True)
    wave(3, True)
    for name in list(copies):
        got(name)

    def back(i):
        for k in range(2):
            d, n = RING[i], i * 2 + k
            if d or k:
                send(f"b{d}{k}", part_ref.at[n], back_ref.at[n], at(dz=d, dc=k))

    wave(2, True)
    for i in range(NZ - 1, NEAR - 1, -1):
        back(i)
    wave(2, False)
    for i in range(NEAR - 1, -1, -1):
        back(i)
    own_part = load(part_ref.at[0], back_ref.at[0], 0)
    own_part.wait()
    for name in list(copies):
        got(name)
    for copy in copies.values():
        copy.wait_send()


def meet(lists, queries, companies):
    return pl.pallas_call(
        meet_kernel,
        out_shape=jax.ShapeDtypeStruct((WORKERS, 8, 128), jnp.float32),
        in_specs=[HBM, HBM, HBM],
        out_specs=VMEM,
        scratch_shapes=[
            pltpu.VMEM((ARTS, LQ, E), jnp.bfloat16),
            pltpu.VMEM((ARTS, E, LQ), jnp.bfloat16),
            pltpu.VMEM((NEAR, 2, ARTS, E, LQ), jnp.bfloat16),
            pltpu.VMEM((NZ - NEAR, 2, ARTS, E, LQ), jnp.bfloat16),
        ]
        + [pltpu.VMEM((C_DEV, LC, E), jnp.bfloat16)] * NY
        + [
            pltpu.VMEM((WORKERS, 8, 128), jnp.int32),
            pltpu.SMEM((WORKERS, 8, 128), jnp.int32),
            pltpu.VMEM((WORKERS, 8, 128), jnp.float32),
            pltpu.SemaphoreType.DMA((N_COPIES,)),
            pltpu.SemaphoreType.DMA((N_COPIES,)),
            pltpu.SemaphoreType.DMA((6,)),
        ],
        compiler_params=pltpu.CompilerParams(
            collective_id=0, has_side_effects=True, vmem_limit_bytes=60 << 20
        ),
    )(lists, queries, companies)


def gather_rows(hot, values, dims):
    total = None
    for _ in range(3):
        head = values.astype(jnp.bfloat16)
        term = lax.dot_general(hot, head, (dims, ((), ())), preferred_element_type=jnp.float32)
        total = term if total is None else total + term
        values = values - head.astype(jnp.float32)
    return total


def finish_kernel(recv_ref, slot_ref, rel_ref, prob_ref):
    lane = lax.broadcasted_iota(jnp.int32, (REQ, 128), 1)
    row = lax.broadcasted_iota(jnp.int32, (REQ, 1), 0)
    slots = slot_ref[...]
    hot_row = jnp.where(lane == slots[:, 0:1], 1.0, 0.0).astype(jnp.bfloat16)
    picked = gather_rows(hot_row, recv_ref[...].reshape(128, 128), ((1,), (0,)))
    score = jnp.sum(jnp.where(lane == slots[:, 64:65], picked, 0.0), axis=1, keepdims=True)
    step = row % (ARTS * PER)
    hot_article = jnp.where(lane == step // PER, 1.0, 0.0).astype(jnp.bfloat16)
    candidate = (row // (ARTS * PER)) * PER + step % PER
    placed = jnp.where(lane == candidate, score, 0.0)
    table = gather_rows(hot_article, placed, ((0,), (0,)))[0:16, 0:NC]
    relevance = table - jnp.sum(table, axis=1, keepdims=True) * (1.0 / NC)
    weights = jnp.exp(TEMPER * relevance)
    probs = weights / jnp.sum(weights, axis=1, keepdims=True)
    rel_ref[...] = relevance[0:ARTS]
    prob_ref[...] = probs[0:ARTS]


def finish(part, slots):
    return pl.pallas_call(
        finish_kernel,
        out_shape=(jax.ShapeDtypeStruct((ARTS, NC), jnp.float32),) * 2,
        in_specs=[VMEM, VMEM],
        out_specs=(VMEM, VMEM),
    )(part, slots)


def per_device(queries, cand_owner, cand_local, companies):
    held = queries.reshape(ARTS, LQ, E)
    owners = jnp.transpose(cand_owner, (0, 2, 1))
    locals_ = jnp.transpose(cand_local, (0, 2, 1))
    lists, slots = make_lists(owners, locals_)
    return finish(meet(lists, held, companies), slots)


def solution(mesh):
    placed = (
        P("art", "seq", None, None),
        P(("art", "seq"), None, None),
        P(("art", "seq"), None, None),
        P("art", None, None),
    )
    return jax.shard_map(
        per_device,
        mesh=mesh,
        in_specs=placed,
        out_specs=(P(("art", "seq"), None), P(("art", "seq"), None)),
        check_vma=False,
    )
```

time: 124 us -> 111 us (0.90)
  local copies, waits for them, and re-layouts: 8.35 us -> 0 us
  Pallas kernels: 115 us -> 110 us
    pallas_call x1, Pallas kernels: 11.4 us -> 4.41 us  [make_lists(): pl.pallas_call(list_kernel, out_shape=(jax.ShapeDtypeStruct((WORKERS, 8,...]
    unnamed x10 -> x0, local copies, waits for them, and re-layouts: 6.52 us -> none
    reshape x2 -> x0, local copies, waits for them, and re-layouts: 1.83 us -> none  [the longest x1 0.92 us: per_device(): cand_owner.reshape(REQ, 1)]
    pallas_call x1, Pallas kernels: 101 us -> 103 us  [meet(): pl.pallas_call(meet_kernel, out_shape=jax.ShapeDtypeStruct((WORKERS, 8, 1...]
where the time goes in v3:
time: 111 us
  Pallas kernels  110 us (99%)
    pallas_call x1, Pallas kernels, meet(): pl.pallas_call(meet_kernel, out_shape=jax.ShapeDtypeStruct((WORKERS, 8, 1...  103 us
    pallas_call x1, Pallas kernels, make_lists(): pl.pallas_call(list_kernel, out_shape=(jax.ShapeDtypeStruct((WORKERS, 8,...  4.41 us
    pallas_call x1, Pallas kernels, finish(): pl.pallas_call(finish_kernel, out_shape=(jax.ShapeDtypeStruct((ARTS, NC),...  3.14 us

profile of v3, /device:TPU:1, one launch (start us, length us, event | category | flops | bytes accessed | tf_op | source)
XLA Modules:
  0.0 111.0 jit_solution(15588679582521210855)
XLA Ops:
  0.6 4.4 %shard_map.59 = (s32[16,8,128]{2,1,0:T(8,128)}, s32[768,128]{1,0:T(8,128)}) custom-call(s32[12,4,16]{2,1,0:T(4,128)} %bitcast.4, s32[12,4,16]{2,1,0:T(4,128)} %bitcast.5), custom_call_target="tpu_custom_call" | custom-call | tf_op jit(solution)/shard_map/pallas_call | solution.py:84
  5.0 102.8 %shard_map.60.recv_ref = f32[16,8,128]{2,1,0:T(8,128)} custom-call(s32[16,8,128]{2,1,0:T(8,128)} %get-tuple-element.4.list_ref, bf16[12,256,128]{2,1,0:T(8,128)(2,1)} %bitcast.3, bf16[256,64,128]{2,1,0:T(8,128)(2,1)} %c_hbm.1), custom_call_target="tpu_custom_call" | custom-call | tf_op jit(solution)/shard_map/pallas_call | solution.py:358
  107.8 3.1 %shard_map.61 = (f32[12,64]{1,0:T(8,128)}, f32[12,64]{1,0:T(8,128)}) custom-call(f32[16,8,128]{2,1,0:T(8,128)} %shard_map.60.recv_ref, s32[768,128]{1,0:T(8,128)} %get-tuple-element.5.slot_ref), custom_call_target="tpu_custom_call" | custom-call | tf_op jit(solution)/shard_map/pallas_call | solution.py:414

commit v4 on v3

--- a/solution.py
+++ b/solution.py
@@ -309,7 +309,7 @@
             score(d, queries, i, base)
             return carry
 
-        lax.fori_loop(0, count, body, 0)
+        lax.fori_loop(0, count, body, 0, unroll=(d == 2))
 
     got("c0", "c1", f"c{NZ - 1}", "c2", f"c{NZ - 2}")
     wave(0, False)
@@ -321,16 +321,16 @@
     got("p31")
     partner(NZ - 3)
     partner(3)
+    got("ups0", "ups1", "upr0", "upr1", "xp20", "xp21", "xm20", "xm21", "xpf2", "xmf2")
+    wave(3, False)
+    got("p40", "m41")
+    partner(4)
+    got(*[n for n in copies if n[0] == "c"])
+    wave(0, True)
+    wave(3, True)
     got("dns0", "dns1", "dnr0", "dnr1", "xp00", "xp01", "xm00", "xm01", "xpf0", "xmf0")
     wave(1, False)
-    got("p40", "m41")
-    partner(4)
-    got("ups0", "ups1", "upr0", "upr1", "xp20", "xp21", "xm20", "xm21", "xpf2", "xmf2")
-    wave(3, False)
-    got(*[n for n in copies if n[0] == "c"])
-    wave(0, True)
     wave(1, True)
-    wave(3, True)
     for name in list(copies):
         got(name)
 

time: 111 us -> 104 us (0.937)
  Pallas kernels: 110 us -> 103 us
    pallas_call x1, Pallas kernels: 103 us -> 95.7 us  [meet(): pl.pallas_call(meet_kernel, out_shape=jax.ShapeDtypeStruct((WORKERS, 8, 1...]
where the time goes in v4:
time: 104 us
  Pallas kernels  103 us (99%)
    pallas_call x1, Pallas kernels, meet(): pl.pallas_call(meet_kernel, out_shape=jax.ShapeDtypeStruct((WORKERS, 8, 1...  95.7 us
    pallas_call x1, Pallas kernels, make_lists(): pl.pallas_call(list_kernel, out_shape=(jax.ShapeDtypeStruct((WORKERS, 8,...  4.41 us
    pallas_call x1, Pallas kernels, finish(): pl.pallas_call(finish_kernel, out_shape=(jax.ShapeDtypeStruct((ARTS, NC),...  3.14 us

profile of v4, /device:TPU:1, one launch (start us, length us, event | category | flops | bytes accessed | tf_op | source)
XLA Modules:
  0.0 103.9 jit_solution(1234604232272169683)
XLA Ops:
  0.6 4.4 %shard_map.59 = (s32[16,8,128]{2,1,0:T(8,128)}, s32[768,128]{1,0:T(8,128)}) custom-call(s32[12,4,16]{2,1,0:T(4,128)} %bitcast.4, s32[12,4,16]{2,1,0:T(4,128)} %bitcast.5), custom_call_target="tpu_custom_call" | custom-call | tf_op jit(solution)/shard_map/pallas_call | solution.py:84
  5.0 95.7 %shard_map.60.recv_ref = f32[16,8,128]{2,1,0:T(8,128)} custom-call(s32[16,8,128]{2,1,0:T(8,128)} %get-tuple-element.4.list_ref, bf16[12,256,128]{2,1,0:T(8,128)(2,1)} %bitcast.3, bf16[256,64,128]{2,1,0:T(8,128)(2,1)} %c_hbm.1), custom_call_target="tpu_custom_call" | custom-call | tf_op jit(solution)/shard_map/pallas_call | solution.py:358
  100.7 3.1 %shard_map.61 = (f32[12,64]{1,0:T(8,128)}, f32[12,64]{1,0:T(8,128)}) custom-call(f32[16,8,128]{2,1,0:T(8,128)} %shard_map.60.recv_ref, s32[768,128]{1,0:T(8,128)} %get-tuple-element.5.slot_ref), custom_call_target="tpu_custom_call" | custom-call | tf_op jit(solution)/shard_map/pallas_call | solution.py:414

commit v5 on v4

--- a/solution.py
+++ b/solution.py
@@ -46,38 +46,47 @@
     return art // (NY * 2), (art // 2) % NY, art % 2, x
 
 
-def column(ref):
-    table = ref[...].reshape(ARTS * PER, ROWS)
-    return jnp.concatenate([table[:, r : r + 1] for r in range(ROWS)], axis=0)
-
-
 def list_kernel(own_ref, loc_ref, list_ref, slot_ref):
     z, y, c, x = place()
-    owner, local = column(own_ref), column(loc_ref)
-    oz, oy, oc = owner // (NY * 2), (owner // 2) % NY, owner % 2
+    owner = own_ref[...].reshape(ARTS * PER, ROWS)
+    local = loc_ref[...].reshape(ARTS * PER, ROWS)
+    oz, oy, oc = owner >> 3, (owner >> 1) & 3, owner & 1
+    dz = (z - oz) & (NZ - 1)
+    ring = jnp.where(dz < NZ // 2, 2 * dz, 2 * (NZ - dz) - 1)
+    side = ring * 2 + ((oc + c) & 1)
+    packed = (((side * 4 + ((oy - y) & 3)) * 64 + (oz * 2 + oc) * NY + oy) * 256) + local
+    packed = jnp.concatenate([packed[:, r : r + 1] for r in range(ROWS)], axis=0)
     lane = lax.broadcasted_iota(jnp.int32, (REQ, 128), 1)
-    row = lax.broadcasted_iota(jnp.int32, (REQ, 1), 0)
-    hot = lane == (oz * 2 + oc) * NY + oy
-    table = jnp.where(hot, 1.0, 0.0).astype(jnp.bfloat16)
-    first = lax.broadcasted_iota(jnp.int32, (REQ, REQ), 0)
-    second = lax.broadcasted_iota(jnp.int32, (REQ, REQ), 1)
+    wide = jnp.broadcast_to(packed, (REQ, 128))
+    hot = lane == ((wide >> 8) & 63)
+    marks = jnp.where(hot, 1.0, 0.0)
+    table = marks.astype(jnp.bfloat16)
+    first = lax.broadcasted_iota(jnp.int32, (128, 128), 0)
+    second = lax.broadcasted_iota(jnp.int32, (128, 128), 1)
     before = jnp.where(second < first, 1.0, 0.0).astype(jnp.bfloat16)
-    counts = jnp.dot(before, table, preferred_element_type=jnp.float32)
-    rank = jnp.sum(jnp.where(hot, counts, 0.0), axis=1, keepdims=True).astype(jnp.int32)
-    article = (row % (ARTS * PER)) // PER
-    spot = ((x - article % NX + NX) % NX) * PART + article // NX
-    value = jnp.where(lane < 64, spot, local)
-    entry = jnp.where(lane % 64 == rank, value, 0).astype(jnp.float32).astype(jnp.bfloat16)
+    seen = jnp.zeros((1, 128), jnp.float32)
+    ranks = []
+    for i in range(REQ // 128):
+        some = slice(i * 128, (i + 1) * 128)
+        counts = jnp.dot(before, table[some], preferred_element_type=jnp.float32) + seen
+        ranks.append(jnp.sum(jnp.where(hot[some], counts, 0.0), axis=1, keepdims=True))
+        seen = seen + jnp.sum(marks[some], axis=0, keepdims=True)
+    rank = jnp.broadcast_to(jnp.concatenate(ranks, axis=0).astype(jnp.int32), (REQ, 128))
+    step = lax.broadcasted_iota(jnp.int32, (ARTS * PER, 128), 0)
+    article = step >> 2
+    spot = ((x - article) & 3) * PART + (article >> 2)
+    spot = jnp.concatenate([spot] * ROWS, axis=0)
+    value = jnp.where(lane < 64, spot, wide & 255)
+    entry = jnp.where((lane & 63) == rank, value, 0).astype(jnp.float32).astype(jnp.bfloat16)
     lists = lax.dot_general(table, entry, (((0,), (0,)), ((), ())), preferred_element_type=jnp.float32)
     lists = lists[: WORKERS * NY].astype(jnp.int32)
     for w in range(WORKERS):
         list_ref[w, 0:NY] = lists[w * NY : (w + 1) * NY]
         list_ref[w, NY:8] = jnp.zeros((8 - NY, 128), jnp.int32)
-    dz = (z - oz + NZ) % NZ
-    ring = jnp.where(dz < NZ // 2, 2 * dz, 2 * (NZ - dz) - 1)
-    side = ring * 2 + jnp.where(oc == c, 0, 1)
-    spot_lane = ((oy - y + NY) % NY) * GROUPS + rank // GROUP
-    slot_ref[...] = jnp.where(lane < 64, side * 8 + rank % GROUP, spot_lane)
+    line = (rank * 43) >> 8
+    slot_ref[...] = jnp.where(
+        lane < 64, (wide >> 16) * 8 + rank - line * GROUP, ((wide >> 14) & 3) * GROUPS + line
+    )
 
 
 def make_lists(owners, locals_):
@@ -381,11 +390,11 @@
     )(lists, queries, companies)
 
 
-def gather_rows(hot, values, dims):
+def gather_rows(hot, values):
     total = None
     for _ in range(3):
         head = values.astype(jnp.bfloat16)
-        term = lax.dot_general(hot, head, (dims, ((), ())), preferred_element_type=jnp.float32)
+        term = jnp.dot(hot, head, preferred_element_type=jnp.float32)
         total = term if total is None else total + term
         values = values - head.astype(jnp.float32)
     return total
@@ -393,21 +402,22 @@
 
 def finish_kernel(recv_ref, slot_ref, rel_ref, prob_ref):
     lane = lax.broadcasted_iota(jnp.int32, (REQ, 128), 1)
-    row = lax.broadcasted_iota(jnp.int32, (REQ, 1), 0)
     slots = slot_ref[...]
     hot_row = jnp.where(lane == slots[:, 0:1], 1.0, 0.0).astype(jnp.bfloat16)
-    picked = gather_rows(hot_row, recv_ref[...].reshape(128, 128), ((1,), (0,)))
+    picked = gather_rows(hot_row, recv_ref[...].reshape(128, 128))
     score = jnp.sum(jnp.where(lane == slots[:, 64:65], picked, 0.0), axis=1, keepdims=True)
-    step = row % (ARTS * PER)
-    hot_article = jnp.where(lane == step // PER, 1.0, 0.0).astype(jnp.bfloat16)
-    candidate = (row // (ARTS * PER)) * PER + step % PER
-    placed = jnp.where(lane == candidate, score, 0.0)
-    table = gather_rows(hot_article, placed, ((0,), (0,)))[0:16, 0:NC]
+    step = lax.broadcasted_iota(jnp.int32, (ARTS * PER, 128), 0)
+    wide = lax.broadcasted_iota(jnp.int32, (ARTS * PER, 128), 1)
+    table = jnp.zeros((ARTS * PER, 128), jnp.float32)
+    for r in range(ROWS):
+        mine = score[r * ARTS * PER : (r + 1) * ARTS * PER]
+        table = jnp.where(wide == r * PER + (step & 3), mine, table)
+    table = jnp.sum(table.reshape(ARTS, PER, 128), axis=1)[:, 0:NC]
     relevance = table - jnp.sum(table, axis=1, keepdims=True) * (1.0 / NC)
     weights = jnp.exp(TEMPER * relevance)
     probs = weights / jnp.sum(weights, axis=1, keepdims=True)
-    rel_ref[...] = relevance[0:ARTS]
-    prob_ref[...] = probs[0:ARTS]
+    rel_ref[...] = relevance
+    prob_ref[...] = probs
 
 
 def finish(part, slots):

time: 104 us -> 101 us (0.971)
  Pallas kernels: 103 us -> 100 us
    pallas_call x1, Pallas kernels: 4.41 us -> 2.29 us  [make_lists(): pl.pallas_call(list_kernel, out_shape=(jax.ShapeDtypeStruct((WORKERS, 8,...]
where the time goes in v5:
time: 101 us
  Pallas kernels  100 us (99%)
    pallas_call x1, Pallas kernels, meet(): pl.pallas_call(meet_kernel, out_shape=jax.ShapeDtypeStruct((WORKERS, 8, 1...  95.7 us
    pallas_call x1, Pallas kernels, make_lists(): pl.pallas_call(list_kernel, out_shape=(jax.ShapeDtypeStruct((WORKERS, 8,...  2.29 us
    pallas_call x1, Pallas kernels, finish(): pl.pallas_call(finish_kernel, out_shape=(jax.ShapeDtypeStruct((ARTS, NC),...  2.27 us

profile of v5, /device:TPU:1, one launch (start us, length us, event | category | flops | bytes accessed | tf_op | source)
XLA Modules:
  0.0 100.9 jit_solution(9855809595404697983)
XLA Ops:
  0.6 2.3 %shard_map.59 = (s32[16,8,128]{2,1,0:T(8,128)}, s32[768,128]{1,0:T(8,128)}) custom-call(s32[12,4,16]{2,1,0:T(4,128)} %bitcast.4, s32[12,4,16]{2,1,0:T(4,128)} %bitcast.5), custom_call_target="tpu_custom_call" | custom-call | tf_op jit(solution)/shard_map/pallas_call | solution.py:93
  2.9 95.7 %shard_map.60.recv_ref = f32[16,8,128]{2,1,0:T(8,128)} custom-call(s32[16,8,128]{2,1,0:T(8,128)} %get-tuple-element.4.list_ref, bf16[12,256,128]{2,1,0:T(8,128)(2,1)} %bitcast.3, bf16[256,64,128]{2,1,0:T(8,128)(2,1)} %c_hbm.1), custom_call_target="tpu_custom_call" | custom-call | tf_op jit(solution)/shard_map/pallas_call | solution.py:367
  98.6 2.3 %shard_map.61 = (f32[12,64]{1,0:T(8,128)}, f32[12,64]{1,0:T(8,128)}) custom-call(f32[16,8,128]{2,1,0:T(8,128)} %shard_map.60.recv_ref, s32[768,128]{1,0:T(8,128)} %get-tuple-element.5.slot_ref), custom_call_target="tpu_custom_call" | custom-call | tf_op jit(solution)/shard_map/pallas_call | solution.py:424

commit v6 on v5

--- a/solution.py
+++ b/solution.py
@@ -46,7 +46,7 @@
     return art // (NY * 2), (art // 2) % NY, art % 2, x
 
 
-def list_kernel(own_ref, loc_ref, list_ref, slot_ref):
+def build(own_ref, loc_ref, list_ref, slot_ref):
     z, y, c, x = place()
     owner = own_ref[...].reshape(ARTS * PER, ROWS)
     local = loc_ref[...].reshape(ARTS * PER, ROWS)
@@ -89,22 +89,10 @@
     )
 
 
-def make_lists(owners, locals_):
-    return pl.pallas_call(
-        list_kernel,
-        out_shape=(
-            jax.ShapeDtypeStruct((WORKERS, 8, 128), jnp.int32),
-            jax.ShapeDtypeStruct((REQ, 128), jnp.int32),
-        ),
-        in_specs=[VMEM, VMEM],
-        out_specs=(VMEM, VMEM),
-    )(owners, locals_)
-
-
 def meet_kernel(
-    list_ref, q_hbm, c_hbm, back_ref,
+    own_ref, loc_ref, q_hbm, c_hbm, back_ref, slot_ref,
     raw_ref, qt_ref, near_ref, far_ref, cat0, cat1, cat2, cat3,
-    lrecv_ref, lists, part_ref, send_sem, recv_sem, local_sem,
+    list_ref, lrecv_ref, lists, part_ref, send_sem, recv_sem, local_sem,
 ):
     slabs = (cat1, cat2, cat3)
     z, y, c, x = place()
@@ -242,6 +230,7 @@
     z_first(1)
     got("e3")
     z_first(3)
+    build(own_ref, loc_ref, list_ref, slot_ref)
     got("ups0", "dns1")
     y_fwd("s", mine)
     for h in (0, 1):
@@ -300,8 +289,8 @@
                 rows = []
                 for u in range(GROUP):
                     slot = g * GROUP + u
-                    query = queries[i, k, lists[w, owner, slot]]
-                    block = cats[d][lists[w, owner, 64 + slot]]
+                    query = queries[i, k, jnp.minimum(lists[w, owner, slot] & 15, ARTS - 1)]
+                    block = cats[d][lists[w, owner, 64 + slot] & (C_DEV - 1)]
                     sims = jnp.dot(block, query, preferred_element_type=jnp.float32)
                     mass = jnp.exp2(sims * (SHARP * math.log2(math.e)))
                     rows.append(jnp.sum(jnp.sum(mass.reshape(8, 8, LQ), axis=0), axis=0, keepdims=True))
@@ -363,12 +352,15 @@
         copy.wait_send()
 
 
-def meet(lists, queries, companies):
+def meet(owners, locals_, queries, companies):
     return pl.pallas_call(
         meet_kernel,
-        out_shape=jax.ShapeDtypeStruct((WORKERS, 8, 128), jnp.float32),
-        in_specs=[HBM, HBM, HBM],
-        out_specs=VMEM,
+        out_shape=(
+            jax.ShapeDtypeStruct((WORKERS, 8, 128), jnp.float32),
+            jax.ShapeDtypeStruct((REQ, 128), jnp.int32),
+        ),
+        in_specs=[VMEM, VMEM, HBM, HBM],
+        out_specs=(VMEM, VMEM),
         scratch_shapes=[
             pltpu.VMEM((ARTS, LQ, E), jnp.bfloat16),
             pltpu.VMEM((ARTS, E, LQ), jnp.bfloat16),
@@ -377,6 +369,7 @@
         ]
         + [pltpu.VMEM((C_DEV, LC, E), jnp.bfloat16)] * NY
         + [
+            pltpu.VMEM((WORKERS, 8, 128), jnp.int32),
             pltpu.VMEM((WORKERS, 8, 128), jnp.int32),
             pltpu.SMEM((WORKERS, 8, 128), jnp.int32),
             pltpu.VMEM((WORKERS, 8, 128), jnp.float32),
@@ -387,7 +380,7 @@
         compiler_params=pltpu.CompilerParams(
             collective_id=0, has_side_effects=True, vmem_limit_bytes=60 << 20
         ),
-    )(lists, queries, companies)
+    )(owners, locals_, queries, companies)
 
 
 def gather_rows(hot, values):
@@ -433,8 +426,7 @@
     held = queries.reshape(ARTS, LQ, E)
     owners = jnp.transpose(cand_owner, (0, 2, 1))
     locals_ = jnp.transpose(cand_local, (0, 2, 1))
-    lists, slots = make_lists(owners, locals_)
-    return finish(meet(lists, held, companies), slots)
+    return finish(*meet(owners, locals_, held, companies))
 
 
 def solution(mesh):

time: 101 us -> 99.8 us (0.988)
    pallas_call x2 -> x1, Pallas kernels: 98 us -> 96.7 us  [meet(): pl.pallas_call(meet_kernel, out_shape=(jax.ShapeDtypeStruct((WORKERS, 8,...]
where the time goes in v6:
time: 99.8 us; the launch traced here: 99.6 us
  Pallas kernels  99 us (99%)
    pallas_call x1, Pallas kernels, meet(): pl.pallas_call(meet_kernel, out_shape=(jax.ShapeDtypeStruct((WORKERS, 8,...  96.7 us
    pallas_call x1, Pallas kernels, finish(): pl.pallas_call(finish_kernel, out_shape=(jax.ShapeDtypeStruct((ARTS, NC),...  2.27 us

profile of v6, /device:TPU:1, one launch (start us, length us, event | category | flops | bytes accessed | tf_op | source)
XLA Modules:
  0.0 99.6 jit_solution(3222166040465914296)
XLA Ops:
  0.6 96.7 %shard_map.59 = (f32[16,8,128]{2,1,0:T(8,128)}, s32[768,128]{1,0:T(8,128)}) custom-call(s32[12,4,16]{2,1,0:T(4,128)} %bitcast.4, s32[12,4,16]{2,1,0:T(4,128)} %bitcast.5, bf16[12,256,128]{2,1,0:T(8,128)(2,1)} %bitcast.3, bf16[256,64,128]{2,1,0:T(8,128)(2,1)} %c_hbm.1), custom_call_target="tpu_custom_call" | custom-call | tf_op jit(solution)/shard_map/pallas_call | solution.py:356
  97.3 2.3 %shard_map.60 = (f32[12,64]{1,0:T(8,128)}, f32[12,64]{1,0:T(8,128)}) custom-call(f32[16,8,128]{2,1,0:T(8,128)} %get-tuple-element.4.recv_ref, s32[768,128]{1,0:T(8,128)} %get-tuple-element.5.slot_ref), custom_call_target="tpu_custom_call" | custom-call | tf_op jit(solution)/shard_map/pallas_call | solution.py:417

commit v7 on v6

--- a/solution.py
+++ b/solution.py
@@ -84,15 +84,16 @@
         list_ref[w, 0:NY] = lists[w * NY : (w + 1) * NY]
         list_ref[w, NY:8] = jnp.zeros((8 - NY, 128), jnp.int32)
     line = (rank * 43) >> 8
-    slot_ref[...] = jnp.where(
+    slots = jnp.where(
         lane < 64, (wide >> 16) * 8 + rank - line * GROUP, ((wide >> 14) & 3) * GROUPS + line
     )
+    slot_ref[...] = slots.astype(jnp.float32).astype(jnp.bfloat16)
 
 
 def meet_kernel(
-    own_ref, loc_ref, q_hbm, c_hbm, back_ref, slot_ref,
+    own_ref, loc_ref, q_hbm, c_hbm, back_ref, slot_hbm,
     raw_ref, qt_ref, near_ref, far_ref, cat0, cat1, cat2, cat3,
-    list_ref, lrecv_ref, lists, part_ref, send_sem, recv_sem, local_sem,
+    slot_ref, list_ref, lrecv_ref, lists, part_ref, send_sem, recv_sem, local_sem,
 ):
     slabs = (cat1, cat2, cat3)
     z, y, c, x = place()
@@ -309,6 +310,7 @@
 
         lax.fori_loop(0, count, body, 0, unroll=(d == 2))
 
+    slots_out = load(slot_ref, slot_hbm, 1)
     got("c0", "c1", f"c{NZ - 1}", "c2", f"c{NZ - 2}")
     wave(0, False)
     got("p30")
@@ -346,6 +348,7 @@
         back(i)
     own_part = load(part_ref.at[0], back_ref.at[0], 0)
     own_part.wait()
+    slots_out.wait()
     for name in list(copies):
         got(name)
     for copy in copies.values():
@@ -357,10 +360,10 @@
         meet_kernel,
         out_shape=(
             jax.ShapeDtypeStruct((WORKERS, 8, 128), jnp.float32),
-            jax.ShapeDtypeStruct((REQ, 128), jnp.int32),
+            jax.ShapeDtypeStruct((REQ, 128), jnp.bfloat16),
         ),
         in_specs=[VMEM, VMEM, HBM, HBM],
-        out_specs=(VMEM, VMEM),
+        out_specs=(VMEM, HBM),
         scratch_shapes=[
             pltpu.VMEM((ARTS, LQ, E), jnp.bfloat16),
             pltpu.VMEM((ARTS, E, LQ), jnp.bfloat16),
@@ -369,6 +372,7 @@
         ]
         + [pltpu.VMEM((C_DEV, LC, E), jnp.bfloat16)] * NY
         + [
+            pltpu.VMEM((REQ, 128), jnp.bfloat16),
             pltpu.VMEM((WORKERS, 8, 128), jnp.int32),
             pltpu.VMEM((WORKERS, 8, 128), jnp.int32),
             pltpu.SMEM((WORKERS, 8, 128), jnp.int32),
@@ -395,7 +399,7 @@
 
 def finish_kernel(recv_ref, slot_ref, rel_ref, prob_ref):
     lane = lax.broadcasted_iota(jnp.int32, (REQ, 128), 1)
-    slots = slot_ref[...]
+    slots = slot_ref[...].astype(jnp.float32).astype(jnp.int32)
     hot_row = jnp.where(lane == slots[:, 0:1], 1.0, 0.0).astype(jnp.bfloat16)
     picked = gather_rows(hot_row, recv_ref[...].reshape(128, 128))
     score = jnp.sum(jnp.where(lane == slots[:, 64:65], picked, 0.0), axis=1, keepdims=True)

time: 99.8 us -> 99.6 us (level)
  no operation moved by 1% of the time
where the time goes in v7:
time: 99.6 us; the launch traced here: 99.4 us
  Pallas kernels  98.8 us (99%)
    pallas_call x1, Pallas kernels, meet(): pl.pallas_call(meet_kernel, out_shape=(jax.ShapeDtypeStruct((WORKERS, 8,...  96.6 us
    pallas_call x1, Pallas kernels, finish(): pl.pallas_call(finish_kernel, out_shape=(jax.ShapeDtypeStruct((ARTS, NC),...  2.2 us

profile of v7, /device:TPU:1, one launch (start us, length us, event | category | flops | bytes accessed | tf_op | source)
XLA Modules:
  0.0 99.4 jit_solution(12366686508063304905)
XLA Ops:
  0.6 96.6 %shard_map.59 = (f32[16,8,128]{2,1,0:T(8,128)}, bf16[768,128]{1,0:T(8,128)(2,1)}) custom-call(s32[12,4,16]{2,1,0:T(4,128)} %bitcast.4, s32[12,4,16]{2,1,0:T(4,128)} %bitcast.5, bf16[12,256,128]{2,1,0:T(8,128)(2,1)} %bitcast.3, bf16[256,64,128]{2,1,0:T(8,128)(2,1)} %c_hbm.1), custom_call_target="tpu_custom_call" | custom-call | tf_op jit(solution)/shard_map/pallas_call | solution.py:359
  97.2 2.2 %shard_map.60 = (f32[12,64]{1,0:T(8,128)}, f32[12,64]{1,0:T(8,128)}) custom-call(f32[16,8,128]{2,1,0:T(8,128)} %get-tuple-element.4.recv_ref, bf16[768,128]{1,0:T(8,128)(2,1)} %get-tuple-element.5.slot_ref), custom_call_target="tpu_custom_call" | custom-call | tf_op jit(solution)/shard_map/pallas_call | solution.py:421
